TPU v7x, 768 devices: a whole 4x8x12 slice. The times are simulated.
768 devices in a mesh: panel: 2 (over core), lat: 12 (over z), lon: 32 (over y, x).
Axes of the slice: x: 4, y: 8, z: 12, core: 2. Of those that a mesh axis runs over, the one named last changes fastest.
Arguments:
- tracers: float32 [2, 4, 8, 96, 4096], P('panel', None, None, 'lat', 'lon'), may hold values from 0.2 to 4
- courant_lon: float32 [2, 8, 96, 4096], P('panel', None, 'lat', 'lon'), may hold values from -0.45 to 0.45
- courant_lat: float32 [2, 8, 96, 4096], P('panel', None, 'lat', 'lon'), may hold values from -0.45 to 0.45
- cell_mass: float32 [2, 8, 96, 4096], P('panel', None, 'lat', 'lon'), as said below
- donor_cell: int32 [2, 12, 32, 12, 64], P('panel', 'lat', 'lon'), may hold values from 0 to 636, as said below
- donor_frac: float32 [2, 2, 12, 32, 12, 64], P(None, 'panel', 'lat', 'lon'), may hold values from 0 to 1
- target_cell: int32 [2, 12, 32, 12, 64], P('panel', 'lat', 'lon'), may hold values from 0 to 1023, as said below
- live_count: int32 [2, 12, 32, 12], P('panel', 'lat', 'lon'), may hold values from 0 to 64, as said below
Outputs:
- updated: float32 [2, 4, 8, 96, 4096], P('panel', None, None, 'lat', 'lon')
Inputs may be any that keep to these rules, and one draw needn't show every extreme that they name: `donor_cell`: entry [p, a, b, d, k] is r * 128 + c with 0 <= r <= 4 and 0 <= c <= 124, so the whole stencil lies in the block of (p, a, b). `target_cell`: entry [p, d, b, s, k] is a flattened cell of the block of (p, d, b); the 768 entries of one device are all distinct. `live_count`: slots k >= the count carry nothing. `cell_mass`: the cell masses are positive.
All inputs are finite; a program needn't handle non-finite values.
Results may differ from a plain program's by a relative error of at most 0.0003.
Values sent between devices are 32-bit elements; how exact they have to be, the bound alone decides.
A program may use at most 32 MiB of HBM per device.

v0:
```python
import jax
import jax.numpy as jnp
from jax import lax
from jax.sharding import Mesh
from jax.sharding import PartitionSpec as P

PANEL_LAT_LON = ("panel", "lat", "lon_0", "lon_1")
LON = ("lon_0", "lon_1")


def by_axis(array, axes):
    for axis in axes:
        array = lax.psum(array, axis)
    return array


def extended(array, sides, width):
    edges = {}
    for axis, dim in sides:
        size, length = (lax.axis_size(axis), array.shape[dim])
        up = [(i, (i + 1) % size) for i in range(size - 1)]
        last = lax.slice_in_dim(array, length - width, length, axis=dim)
        leading = lax.slice_in_dim(array, 0, width, axis=dim)
        edges[dim] = (
            lax.ppermute(last, axis, up),
            lax.ppermute(leading, axis, [(b, a) for a, b in up]),
        )
    done = []
    for _, dim in sides:
        low, high = edges[dim]
        around = [(width, width) if d in done else (0, 0) for d in range(array.ndim)]
        array = jnp.concatenate([jnp.pad(low, around), array, jnp.pad(high, around)], axis=dim)
        done.append(dim)
    return array


def swapped(array, axis, apart):
    return lax.ppermute(array, axis, [(i, i ^ 1 << apart) for i in range(lax.axis_size(axis))])


def cut(source, begin_at, end_at, dim_index):
    return lax.slice_in_dim(source, begin_at, end_at, axis=dim_index)


def face_flux(padded_field, courant, length, from_end):
    dim_index = padded_field.ndim - from_end
    edge_values = 7.0 / 12.0 * (
        cut(padded_field, 1, length + 4, dim_index) + cut(padded_field, 2, length + 5, dim_index)
    ) - 1.0 / 12.0 * (
        cut(padded_field, 0, length + 3, dim_index) + cut(padded_field, 3, length + 6, dim_index)
    )
    edge_left = cut(edge_values, 0, length + 1, dim_index)
    edge_middle = cut(edge_values, 1, length + 2, dim_index)
    edge_right = cut(edge_values, 2, length + 3, dim_index)
    cell_left = cut(padded_field, 2, length + 3, dim_index)
    cell_right = cut(padded_field, 3, length + 4, dim_index)
    number = cut(courant, 3, length + 4, dim_index)
    slope_left = edge_middle - edge_left
    curve_left = 6.0 * (cell_left - 0.5 * (edge_left + edge_middle))
    flux_positive = number * (
        edge_middle - 0.5 * number * (slope_left - (1.0 - 2.0 / 3.0 * number) * curve_left)
    )
    reverse_speed = -number
    slope_right = edge_right - edge_middle
    curve_right = 6.0 * (cell_right - 0.5 * (edge_middle + edge_right))
    flux_negative = number * (
        edge_middle
        + 0.5 * reverse_speed * (slope_right + (1.0 - 2.0 / 3.0 * reverse_speed) * curve_right)
    )
    return jnp.where(number > 0.0, flux_positive, flux_negative)


def advect(padded_field, zonal_padded, meridional_padded):
    row_total = padded_field.shape[-2] - 6
    column_total = padded_field.shape[-1] - 6
    zonal_flux = face_flux(
        padded_field[..., 3 : 3 + row_total, :],
        zonal_padded[..., 3 : 3 + row_total, :],
        column_total,
        1,
    )
    meridional_flux = face_flux(
        padded_field[..., 3 : 3 + column_total],
        meridional_padded[..., 3 : 3 + column_total],
        row_total,
        2,
    )
    center = padded_field[..., 3 : 3 + row_total, 3 : 3 + column_total]
    return (
        center
        - (zonal_flux[..., 1:] - zonal_flux[..., :-1])
        - (meridional_flux[..., 1:, :] - meridional_flux[..., :-1, :])
    )


def cubic_weights(fraction):
    return jnp.stack(
        [
            -fraction * (fraction - 1.0) * (fraction - 2.0) / 6.0,
            (fraction + 1.0) * (fraction - 1.0) * (fraction - 2.0) / 2.0,
            -(fraction + 1.0) * fraction * (fraction - 2.0) / 2.0,
            (fraction + 1.0) * fraction * (fraction - 1.0) / 6.0,
        ],
        axis=-1,
    )


def interpolate(flat_field, base_cell, fraction_row, fraction_column, column_total):
    row_weights = cubic_weights(fraction_row)
    column_weights = cubic_weights(fraction_column)
    point_count = base_cell.shape[0]
    stencil_rows = jnp.arange(4, dtype=jnp.int32)[:, None] * column_total
    stencil_columns = jnp.arange(4, dtype=jnp.int32)[None, :]
    offsets = (stencil_rows + stencil_columns).reshape(16)
    spots = (offsets[:, None] + base_cell[None, :]).reshape(-1)
    factors = (row_weights[:, :, None] * column_weights[:, None, :]).reshape(point_count, 16).T
    picked = jnp.take(flat_field, spots, axis=1).reshape(flat_field.shape[0], 16, point_count)
    return jnp.sum(factors[None] * picked, axis=1)


def body(
    tracers, courant_lon, courant_lat, cell_mass, donor_cell, donor_frac, target_cell, live_count
):
    tracer_field = tracers[0]
    tracer_count, level_count, row_total, column_total = tracer_field.shape
    mass_weights = cell_mass[0]
    mass_old = by_axis(jnp.sum(mass_weights[None] * tracer_field, axis=(1, 2, 3)), PANEL_LAT_LON)
    stacked = jnp.concatenate([tracer_field, courant_lon, courant_lat], axis=0)
    padded = extended(stacked, (("lat", 2), (LON, 3)), 3)
    padded_field = padded[:tracer_count]
    zonal_padded = padded[tracer_count : tracer_count + 1]
    meridional_padded = padded[tracer_count + 1 :]
    advected = advect(padded_field, zonal_padded, meridional_padded)
    stack_rows = tracer_count * level_count
    cell_total = row_total * column_total
    flat_field = advected.reshape(stack_rows, cell_total)
    row_blocks = donor_cell.shape[3]
    capacity = donor_cell.shape[4]
    payload = interpolate(
        flat_field,
        donor_cell.reshape(-1),
        donor_frac[0].reshape(-1),
        donor_frac[1].reshape(-1),
        column_total,
    )
    halfway = lax.all_to_all(payload, "lat", split_axis=1, concat_axis=1, tiled=True)
    arrived = swapped(halfway, "panel", 0)
    live_slots = jnp.arange(capacity, dtype=jnp.int32)[None, :] < live_count.reshape(row_blocks, 1)
    target_spots = jnp.where(
        live_slots, target_cell.reshape(row_blocks, capacity), cell_total
    ).reshape(-1)
    merged = flat_field.at[:, target_spots].set(arrived, mode="drop")
    intersected = merged.reshape(tracer_count, level_count, row_total, column_total)
    local_after = jnp.sum(mass_weights[None] * intersected, axis=(1, 2, 3))
    mass_new = by_axis(local_after, PANEL_LAT_LON)
    return (intersected * (mass_old / mass_new)[:, None, None, None])[None]


def solution(mesh):
    split = Mesh(
        mesh.devices.reshape(mesh.shape["panel"], mesh.shape["lat"], 8, 4),
        ("panel", "lat", "lon_0", "lon_1"),
    )
    placed = (
        P("panel", None, None, "lat", LON),
        P("panel", None, "lat", LON),
        P("panel", None, "lat", LON),
        P("panel", None, "lat", LON),
        P("panel", "lat", LON, None, None),
        P(None, "panel", "lat", LON, None, None),
        P("panel", "lat", LON, None, None),
        P("panel", "lat", LON, None),
    )
    return jax.shard_map(
        body,
        mesh=split,
        in_specs=placed,
        out_specs=P("panel", None, None, "lat", LON),
        check_vma=False,
    )
```

profile of v0, /device:TPU:2, one launch (start us, length us, event | category | flops | bytes accessed | tf_op | source)
XLA Modules:
  0.0 166.1 jit_solution(1157557414969570072)
XLA Ops:
  0.0 1.0 pad_maximum_fusion.18
  1.0 1.3 collective-permute-start.1
  2.3 4.9 %collective-permute-start = (f32[6,8,3,128]{3,2,1,0:T(4,128)S(1)}, f32[6,8,3,128]{3,2,1,0:T(4,128)S(1)}, u32[]{:S(2)}, u32[]{:S(2)}) collective-permute-start(f32[6,8,3,128]{3,2,1,0:T(4,128)S(1)} %get-tuple-element.23), channel_id=1, source_target_pairs={{0,32},{32,64},{64,96},{96,128},{128,160},{160,192},{192,224},{224... | collective-permute-start | bytes 221192 | tf_op jit(solution)/shard_map/ppermute | solution.py:25
  7.3 0.1 fusion.38
  7.4 11.1 %collective-permute-start.2 = (f32[6,8,8,3]{3,2,1,0:T(8,128)S(1)}, f32[6,8,8,3]{3,2,1,0:T(8,128)S(1)}, u32[]{:S(2)}, u32[]{:S(2)}) collective-permute-start(f32[6,8,8,3]{3,2,1,0:T(8,128)S(1)} %get-tuple-element.20), channel_id=1, source_target_pairs={{1,0},{2,1},{3,2},{4,3},{5,4},{6,5},{7,6},{8,7},{9,8},{10,9},{11,1... | collective-permute-start | bytes 13832 | tf_op jit(solution)/shard_map/ppermute | solution.py:26
  18.5 1.9 %collective-permute-start.3 = (f32[6,8,8,3]{3,2,1,0:T(8,128)S(1)}, f32[6,8,8,3]{3,2,1,0:T(8,128)S(1)}, u32[]{:S(2)}, u32[]{:S(2)}) collective-permute-start(f32[6,8,8,3]{3,2,1,0:T(8,128)S(1)} %get-tuple-element.19), channel_id=1, source_target_pairs={{0,1},{1,2},{2,3},{3,4},{4,5},{5,6},{6,7},{7,8},{8,9},{9,10},{10,1... | collective-permute-start | bytes 13832 | tf_op jit(solution)/shard_map/ppermute | solution.py:25
  20.4 0.7 reduce.6
  21.1 0.1 add.262
  21.2 0.1 iota_add_fusion
  21.3 0.1 add.260
  21.3 0.1 add_bitcast_fusion
  21.4 0.1 copy.38
  21.5 0.1 compare_select_fusion
  21.6 0.7 slice_reduce_fusion.1
  22.3 0.1 reshape_squeeze.6
  22.4 0.1 reshape_squeeze.7
  22.5 0.0 copy-start.3
  22.6 0.1 fusion.36
  22.7 0.0 collective-permute-done.2
  22.7 3.3 %collective-permute-done.3 = f32[6,8,8,3]{3,2,1,0:T(8,128)S(1)} collective-permute-done((f32[6,8,8,3]{3,2,1,0:T(8,128)S(1)}, f32[6,8,8,3]{3,2,1,0:T(8,128)S(1)}, u32[]{:S(2)}, u32[]{:S(2)}) %collective-permute-start.3) | collective-permute-done | bytes 4640 | tf_op jit(solution)/shard_map/ppermute | solution.py:25
  26.1 0.0 collective-permute-done.1
  26.1 0.0 collective-permute-done
  26.1 0.8 compare_bitcast_fusion.1
  26.9 0.8 compare_bitcast_fusion
  27.7 1.1 maximum_maximum_fusion
  28.9 0.0 copy-done
  28.9 0.0 copy-done.1
  28.9 0.0 copy-done.2
  28.9 0.1 pad_maximum_fusion
  29.0 0.1 fusion.12
  29.1 0.2 fusion.5
  29.3 0.6 fusion.28
  29.9 0.4 fusion.20
  30.3 0.0 copy-done.3
  30.3 0.1 multiply_reduce_fusion.2
  30.5 0.2 copy.31
  30.7 41.0 %gather_fusion = f32[12288,32]{1,0:T(8,128)} fusion(f32[32,1024]{0,1:T(8,128)S(1)} %copy.31, s32[12288]{0:T(1024)S(1)} %broadcast_clamp_fusion), kind=kCustom, calls=%fused_computation | custom fusion | bytes 3194880 | tf_op jit(solution)/shard_map/jit(_take)/gather | solution.py:117
  71.7 8.9 %multiply_reduce_fusion = f32[32,768]{0,1:T(8,128)S(1)} fusion(f32[32,16,768]{0,2,1:T(8,128)} %bitcast.59, f32[16,768]{1,0:T(8,128)S(1)} %bitcast.75, pred[16,768]{1,0:T(8,128)(4,1)S(1)} %fusion.36), kind=kLoop, calls=%fused_computation.2 | loop fusion | flops 1155072 | bytes 1732608 | tf_op jit(solution)/shard_map/reduce_sum | solution.py:118
  80.6 0.2 copy.29
  80.8 0.8 reshape.388
  81.6 7.5 %all-to-all-start = ((f32[12,1,2048]{2,1,0:T(1,128)}), f32[12,1,2048]{2,1,0:T(1,128)S(1)}, u32[]{:S(2)}, u32[]{:S(2)}) async-start(f32[12,1,2048]{2,1,0:T(1,128)} %reshape.388), calls=%async_computation | async-start | bytes 196608 | tf_op jit(solution)/shard_map/all_to_all | solution.py:146
  89.2 0.1 reshape.365
  89.2 0.1 iota_compare_fusion
  89.3 0.1 lt.65
  89.4 11.3 %all-to-all-done = f32[12,1,2048]{2,1,0:T(1,128)S(1)} async-done(((f32[12,1,2048]{2,1,0:T(1,128)}), f32[12,1,2048]{2,1,0:T(1,128)S(1)}, u32[]{:S(2)}, u32[]{:S(2)}) %all-to-all-start) | async-done | bytes 98336 | tf_op jit(solution)/shard_map/all_to_all | solution.py:146
  100.7 0.5 broadcast.378
  101.3 0.9 reduce.10
  102.1 0.1 reshape.389
  102.2 0.1 copy.30
  102.4 0.1 all_to_all.10
  102.5 1.9 %collective-permute-start.4 = (f32[32,768]{1,0:T(8,128)S(1)}, f32[32,768]{1,0:T(8,128)S(1)}, u32[]{:S(2)}, u32[]{:S(2)}) collective-permute-start(f32[32,768]{1,0:T(8,128)S(1)} %all_to_all.10), channel_id=1, source_target_pairs={{0,384},{384,0},{1,385},{385,1},{2,386},{386,2},{3,387},{387,3},{4... | collective-permute-start | bytes 294920 | tf_op jit(solution)/shard_map/ppermute | solution.py:38
  104.4 0.2 copy.34
  104.7 1.0 collective-permute-done.4
  105.7 0.2 copy.32
  105.8 4.4 %scatter_fusion = f32[32,1024]{0,1:T(8,128)S(1)} fusion(f32[32,1024]{0,1:T(8,128)S(1)} %copy.31, s32[768]{0:T(1024)S(1)} %fusion.37, f32[768,32]{1,0:T(8,128)S(1)} %copy.32), kind=kCustom, calls=%fused_computation.1 | custom fusion | bytes 297984 | tf_op jit(solution)/shard_map/scatter | solution.py:152
  110.2 0.2 copy.33
  110.4 0.2 multiply_reduce_fusion.1
  110.5 0.1 reduce_sum.37
  110.6 0.1 reduce_sum.38
  110.8 2.5 %all-reduce.5 = (f32[4]{0:T(128)S(1)}, f32[4]{0:T(128)S(1)}) all-reduce(f32[4]{0:T(128)S(1)} %get-tuple-element.25, f32[4]{0:T(128)S(1)} %reduce_sum.38), channel_id=1, replica_groups=mesh['panel'=2,'lat'=12,'lon_0'=8,'lon_1'=4] {'panel'}, use_global_device_ids=true, to_apply=%region_3.0 | all-reduce | flops 8 | bytes 64 | tf_op jit(solution)/shard_map/psum | solution.py:13
  113.2 21.1 %all-reduce.2 = (f32[4]{0:T(128)S(1)}, f32[4]{0:T(128)S(1)}) all-reduce(f32[4]{0:T(128)S(1)} %get-tuple-element.13, f32[4]{0:T(128)S(1)} %get-tuple-element.14), channel_id=1, replica_groups=mesh['panel'=2,'lat'=12,'lon_0'=8,'lon_1'=4] {'lat'}, use_global_device_ids=true, to_apply=%region_4.0 | all-reduce | flops 8 | bytes 64 | tf_op jit(solution)/shard_map/psum | solution.py:13
  134.4 19.4 %all-reduce.3 = (f32[4]{0:T(128)S(1)}, f32[4]{0:T(128)S(1)}) all-reduce(f32[4]{0:T(128)S(1)} %get-tuple-element.7, f32[4]{0:T(128)S(1)} %get-tuple-element.8), channel_id=1, replica_groups=mesh['panel'=2,'lat'=12,'lon_0'=8,'lon_1'=4] {'lon_0'}, use_global_device_ids=true, to_apply=%region_5.6 | all-reduce | flops 8 | bytes 64 | tf_op jit(solution)/shard_map/psum | solution.py:13
  153.8 11.6 %all-reduce.4 = (f32[4]{0:T(128)S(1)}, f32[4]{0:T(128)S(1)}) all-reduce(f32[4]{0:T(128)S(1)} %get-tuple-element.9, f32[4]{0:T(128)S(1)} %get-tuple-element.10), channel_id=1, replica_groups=mesh['panel'=2,'lat'=12,'lon_0'=8,'lon_1'=4] {'lon_1'}, use_global_device_ids=true, to_apply=%region_6.7 | all-reduce | flops 8 | bytes 64 | tf_op jit(solution)/shard_map/psum | solution.py:13
  165.4 0.7 bitcast_multiply_fusion
  (24 shorter events, 0.4 us)
Async XLA Ops:
  0.0 28.9 %copy-start = (f32[1,4,8,8,128]{4,3,2,1,0:T(8,128)S(1)}, f32[1,4,8,8,128]{4,3,2,1,0:T(8,128)}, u32[]{:S(2)}) copy-start(f32[1,4,8,8,128]{4,3,2,1,0:T(8,128)} %param.8) | copy-start | bytes 393220
  0.0 28.9 %copy-start.1 = (f32[1,8,8,128]{3,2,1,0:T(8,128)S(1)}, f32[1,8,8,128]{3,2,1,0:T(8,128)}, u32[]{:S(2)}) copy-start(f32[1,8,8,128]{3,2,1,0:T(8,128)} %param.10) | copy-start | bytes 98308
  0.0 28.9 %copy-start.2 = (f32[1,8,8,128]{3,2,1,0:T(8,128)S(1)}, f32[1,8,8,128]{3,2,1,0:T(8,128)}, u32[]{:S(2)}) copy-start(f32[1,8,8,128]{3,2,1,0:T(8,128)} %param.9) | copy-start | bytes 98308
  1.0 25.0 %collective-permute-start.1 = (f32[6,8,3,128]{3,2,1,0:T(4,128)S(1)}, f32[6,8,3,128]{3,2,1,0:T(4,128)S(1)}, u32[]{:S(2)}, u32[]{:S(2)}) collective-permute-start(f32[6,8,3,128]{3,2,1,0:T(4,128)S(1)} %get-tuple-element.24), channel_id=1, source_target_pairs={{32,0},{64,32},{96,64},{128,96},{160,128},{192,160},{224,192},{256... | collective-permute-start | bytes 221192 | tf_op jit(solution)/shard_map/ppermute | solution.py:26
  2.3 23.7 %collective-permute-start = (f32[6,8,3,128]{3,2,1,0:T(4,128)S(1)}, f32[6,8,3,128]{3,2,1,0:T(4,128)S(1)}, u32[]{:S(2)}, u32[]{:S(2)}) collective-permute-start(f32[6,8,3,128]{3,2,1,0:T(4,128)S(1)} %get-tuple-element.23), channel_id=1, source_target_pairs={{0,32},{32,64},{64,96},{96,128},{128,160},{160,192},{192,224},{224... | collective-permute-start | bytes 221192 | tf_op jit(solution)/shard_map/ppermute | solution.py:25
  7.4 15.3 %collective-permute-start.2 = (f32[6,8,8,3]{3,2,1,0:T(8,128)S(1)}, f32[6,8,8,3]{3,2,1,0:T(8,128)S(1)}, u32[]{:S(2)}, u32[]{:S(2)}) collective-permute-start(f32[6,8,8,3]{3,2,1,0:T(8,128)S(1)} %get-tuple-element.20), channel_id=1, source_target_pairs={{1,0},{2,1},{3,2},{4,3},{5,4},{6,5},{7,6},{8,7},{9,8},{10,9},{11,1... | collective-permute-start | bytes 13832 | tf_op jit(solution)/shard_map/ppermute | solution.py:26
  18.5 7.6 %collective-permute-start.3 = (f32[6,8,8,3]{3,2,1,0:T(8,128)S(1)}, f32[6,8,8,3]{3,2,1,0:T(8,128)S(1)}, u32[]{:S(2)}, u32[]{:S(2)}) collective-permute-start(f32[6,8,8,3]{3,2,1,0:T(8,128)S(1)} %get-tuple-element.19), channel_id=1, source_target_pairs={{0,1},{1,2},{2,3},{3,4},{4,5},{5,6},{6,7},{7,8},{8,9},{9,10},{10,1... | collective-permute-start | bytes 13832 | tf_op jit(solution)/shard_map/ppermute | solution.py:25
  22.5 7.8 %copy-start.3 = (f32[1,8,8,128]{3,2,1,0:T(8,128)S(1)}, f32[1,8,8,128]{3,2,1,0:T(8,128)}, u32[]{:S(2)}) copy-start(f32[1,8,8,128]{3,2,1,0:T(8,128)} %param.11) | copy-start | bytes 98308
  71.7 17.4 %copy-start.4 = (s32[1,1,1,12,64]{4,2,3,1,0:T(1,128)S(1)}, s32[1,1,1,12,64]{4,2,3,1,0:T(1,128)}, u32[]{:S(2)}) copy-start(s32[1,1,1,12,64]{4,2,3,1,0:T(1,128)} %param.14) | copy-start | bytes 9220
  71.7 17.5 %copy-start.5 = (s32[1,1,1,12]{3,2,1,0:T(1,128)S(1)}, s32[1,1,1,12]{3,2,1,0:T(1,128)}, u32[]{:S(2)}) copy-start(s32[1,1,1,12]{3,2,1,0:T(1,128)} %param.15) | copy-start | bytes 148
  81.6 19.1 %all-to-all-start = ((f32[12,1,2048]{2,1,0:T(1,128)}), f32[12,1,2048]{2,1,0:T(1,128)S(1)}, u32[]{:S(2)}, u32[]{:S(2)}) async-start(f32[12,1,2048]{2,1,0:T(1,128)} %reshape.388), calls=%async_computation | async-start | bytes 196608 | tf_op jit(solution)/shard_map/all_to_all | solution.py:146
  102.5 3.2 %collective-permute-start.4 = (f32[32,768]{1,0:T(8,128)S(1)}, f32[32,768]{1,0:T(8,128)S(1)}, u32[]{:S(2)}, u32[]{:S(2)}) collective-permute-start(f32[32,768]{1,0:T(8,128)S(1)} %all_to_all.10), channel_id=1, source_target_pairs={{0,384},{384,0},{1,385},{385,1},{2,386},{386,2},{3,387},{387,3},{4... | collective-permute-start | bytes 294920 | tf_op jit(solution)/shard_map/ppermute | solution.py:38
where the time goes:
time: 167 us; the launch traced here: 166 us
  blocking collectives  54.6 us (33%)
  local copies, waits for them, and re-layouts  49.6 us (30%)
  starting transfers between devices  28.6 us (17%)
  other arithmetic  17.3 us (10%)
  waiting for transfers between devices  15.6 us (9%)
    psum x4, blocking collectives, by_axis(): array = lax.psum(array, axis)  54.6 us
    gather x1, local copies, waits for them, and re-layouts, interpolate(): jnp.take(flat_field, spots, axis=1)  41 us
    ppermute x2, starting transfers between devices, extended(): lax.ppermute(leading, axis, [(b, a) for a, b in up])  12.4 us
    all_to_all x1, waiting for transfers between devices, body(): lax.all_to_all(payload, 'lat', split_axis=1, concat_axis=1, tiled=True)  11.3 us
    reduce_sum x1, other arithmetic, interpolate(): return jnp.sum(factors[None] * picked, axis=1)  8.92 us
    all_to_all x1, starting transfers between devices, body(): lax.all_to_all(payload, 'lat', split_axis=1, concat_axis=1, tiled=True)  7.52 us
    ppermute x2, starting transfers between devices, extended(): lax.ppermute(last, axis, up)  6.83 us
    scatter x2, local copies, waits for them, and re-layouts, body(): merged = flat_field.at[:, target_spots].set(arrived, mode='drop')  4.56 us
  transfers between devices with their start and end apart: 6, of which 3 were waited for; matrix products, arithmetic and copies ran while one was open for 2% of the time, Pallas kernels for 0%

commit v1 on v0

v1 whole, which is shorter than its diff:
```python
import jax
import jax.numpy as jnp
from jax import lax
from jax.experimental import pallas as pl
from jax.experimental.pallas import tpu as pltpu
from jax.sharding import PartitionSpec as P

F32 = jnp.float32
BF16 = jnp.bfloat16
MESH = pl.DeviceIdType.MESH

T = 4
L = 8
F = T * L
R = 8
C = 128
K = 64
NX = 4
WEST, EAST, SOUTH, NORTH, NORTH_C, MASSES, MARGIN, SUM_X, SUM_Y, SUM_Z = range(10)


def left(x, by):
    by = by % C
    return x if by == 0 else pltpu.roll(x, (C - by) % C, x.ndim - 1)


def alphas(c):
    s = jnp.abs(c)
    m = 0.5 * s
    n = m - m * s * (2.0 / 3.0)
    n3 = 3.0 * n
    k1 = c * (1.0 - m - n3)
    k0 = c * (m - n3)
    ka = 2.0 * n3 * c
    u = k0 * (1.0 / 12.0)
    w = k1 * (1.0 / 12.0)
    pos = c > 0.0
    zero = jnp.zeros_like(c)
    near = 7.0 * (u + w) + ka
    far = 7.0 * u - w
    mid = 7.0 * w - u
    return (
        jnp.where(pos, -u, zero),
        jnp.where(pos, far, -w),
        jnp.where(pos, near, mid),
        jnp.where(pos, mid, near),
        jnp.where(pos, -w, far),
        jnp.where(pos, zero, -u),
    )


def betas(c, c_next):
    here, after = alphas(c), alphas(c_next)
    return [-here[0]] + [after[k - 1] - here[k] for k in range(1, 6)] + [after[5]]


def cubic(t):
    a, b, d = t + 1.0, t - 1.0, t - 2.0
    return (
        -t * b * d * (1.0 / 6.0),
        a * b * d * 0.5,
        -a * t * d * 0.5,
        a * t * b * (1.0 / 6.0),
    )


def pick(delta, weights):
    value = jnp.where(delta == 0, weights[0], 0.0)
    for i in range(1, 4):
        value = jnp.where(delta == i, weights[i], value)
    return value


def halves(x):
    high = x.astype(BF16)
    return high, (x - high.astype(F32)).astype(BF16)


def wait_all(ref, sem):
    pltpu.make_async_copy(ref, ref, sem).wait()


def kernel(nz, nlon, q_hbm, clon_hbm, clat_hbm, mass_hbm, donor_hbm, frac_hbm, target_hbm, live,
           out, field, clon, clat, mass, donor, frac, target, send_w, send_e, recv_w, recv_e,
           cm_send, cm_recv, packet, arrived, rows, sum_x, sum_y, sum_z, base, adv, onehot, colw,
           roww, lhs, mixed, scat_hi, scat_lo, rowmask, scattered, local_sem, send_sem, recv_sem):
    p = lax.axis_index("panel")
    z = lax.axis_index("lat")
    b = lax.axis_index("lon")
    x, y = lax.rem(b, NX), lax.div(b, NX)
    ny = nlon // NX
    other = 1 - p

    def at_z(step):
        return lax.rem(z + step, nz)

    def at_x(step):
        return y * NX + lax.rem(x + step, NX)

    def at_y(step):
        return lax.rem(y + step, ny) * NX + x

    west, east = lax.rem(b + nlon - 1, nlon), lax.rem(b + 1, nlon)
    south, north = at_z(nz - 1), at_z(1)

    loads = [
        pltpu.make_async_copy(q_hbm, field.at[:, pl.ds(R, R), :], local_sem.at[0]),
        pltpu.make_async_copy(clon_hbm, clon, local_sem.at[1]),
        pltpu.make_async_copy(clat_hbm, clat.at[:, pl.ds(0, R), :], local_sem.at[2]),
        pltpu.make_async_copy(mass_hbm, mass, local_sem.at[3]),
        pltpu.make_async_copy(donor_hbm, donor, local_sem.at[4]),
        pltpu.make_async_copy(frac_hbm, frac, local_sem.at[5]),
        pltpu.make_async_copy(target_hbm, target, local_sem.at[6]),
    ]
    barrier = pltpu.get_barrier_semaphore()
    partners = [(other, at_z(i), b) for i in range(nz)] + [(p, at_z(i), b) for i in range(1, nz)]
    partners += [(p, z, west), (p, z, east)]
    partners += [(core, z, at_x(i)) for i in range(1, NX) for core in (p, other)]
    partners += [(p, z, at_y(i)) for i in range(1, ny)]
    for partner in partners:
        pl.semaphore_signal(barrier, inc=1, device_id=partner, device_id_type=MESH)
    for load in loads:
        load.start()

    lane = lax.broadcasted_iota(jnp.int32, (R, C), 1)
    lane16 = lax.broadcasted_iota(jnp.int32, (2 * R, C), 1)
    lane_row = lax.broadcasted_iota(jnp.int32, (1, C), 1)
    sub = lax.broadcasted_iota(jnp.int32, (2 * R, C), 0)
    column = lax.broadcasted_iota(jnp.int32, (C, C), 0)
    low, low16 = lane < K, lane16 < K

    loads[6].wait()
    spots = jnp.concatenate([target[0:6, :], target[6:12, :]], axis=1)
    spot_col = spots & (C - 1)
    spot_row = spots >> 7
    live_rows = []
    for v in range(6):
        count = jnp.where(lane_row < K, live[v], live[v + 6])
        live_rows.append(jnp.where((lane_row & (K - 1)) < count, spot_row[v : v + 1, :], R))
    for v in range(6):
        cols = pl.ds(v * C, C)
        onehot[:, cols] = jnp.where(column == spot_col[v : v + 1, :], 1.0, 0.0).astype(BF16)
        rowmask[:, cols] = jnp.where(sub == live_rows[v], 1.0, 0.0).astype(BF16)
    filled = lax.dot_general(
        rowmask[...], onehot[...], (((1,), (1,)), ((), ())), preferred_element_type=F32
    )[0:R, :]

    loads[3].wait()
    by_row = jnp.concatenate([mass[pl.ds(r, L, stride=R), :] for r in range(R)], axis=0)
    mass_hi, mass_lo = halves(by_row)
    mass_at = jnp.dot(mass_hi, onehot[...], preferred_element_type=F32) + jnp.dot(
        mass_lo, onehot[...], preferred_element_type=F32
    )
    for v in range(6):
        total = jnp.zeros((L, C), F32)
        for r in range(R):
            total += jnp.where(
                live_rows[v] == r, mass_at[r * L : (r + 1) * L, v * C : (v + 1) * C], 0.0
            )
        turned = left(total, K)
        cm_send[v] = jnp.where(low, total, pltpu.roll(turned, 4, 0))[0:4, :]
        cm_send[v + 6] = jnp.where(low, turned, pltpu.roll(total, 4, 0))[0:4, :]

    loads[0].wait()
    loads[1].wait()
    own = [jnp.zeros((R, C), F32) for _ in range(4)]
    firsts = (0, 4, 124, 120)
    for f in range(F):
        tile = field[f, R : 2 * R, :]
        band = (lane >= 4 * f) & (lane < 4 * f + 4)
        own = [jnp.where(band, left(tile, first - 4 * f), o) for first, o in zip(firsts, own)]
    own_w, own_w2, own_e, own_e2 = own
    edge = [jnp.zeros((R, C), F32) for _ in range(4)]
    firsts = (0, 1, 124, 125)
    for l in range(L):
        tile = clon[l]
        band = (lane >= 4 * l) & (lane < 4 * l + 4)
        edge = [jnp.where(band, left(tile, first - 4 * l), o) for first, o in zip(firsts, edge)]
    edge = [o + pltpu.roll(o, 32, 1) for o in edge]
    c_w, c_w_next, c_e, c_e_next = [o + pltpu.roll(o, 64, 1) for o in edge]
    send_w[0] = own_w
    send_w[1] = c_w
    send_e[0] = own_e

    loads[4].wait()
    loads[5].wait()
    cells = jnp.concatenate([donor[0:6, :], donor[6:12, :]], axis=1)
    start_col = cells & (C - 1)
    start_row = cells >> 7
    row_weights = cubic(jnp.concatenate([frac[0, 0:6, :], frac[0, 6:12, :]], axis=1))
    col_weights = cubic(jnp.concatenate([frac[1, 0:6, :], frac[1, 6:12, :]], axis=1))
    for r in range(R):
        roww[r, 0:6, :] = pick(r - start_row, row_weights)
    for v in range(6):
        cols = pl.ds(v * C, C)
        weights = pick(
            column - start_col[v : v + 1, :], [w[v : v + 1, :] for w in col_weights]
        )
        high, low_part = halves(weights)
        colw[0:C, cols] = high
        colw[C : 2 * C, cols] = high
        colw[2 * C : 3 * C, cols] = low_part

    pl.semaphore_wait(barrier, len(partners))

    def remote(src, dst, which, device):
        return pltpu.make_async_remote_copy(
            src_ref=src,
            dst_ref=dst,
            send_sem=send_sem.at[which],
            recv_sem=recv_sem.at[which],
            device_id=device,
            device_id_type=MESH,
        )

    halo = [
        remote(send_w, recv_e, EAST, (p, z, west)),
        remote(send_e, recv_w, WEST, (p, z, east)),
        remote(q_hbm.at[:, pl.ds(5, 3), :], field.at[:, pl.ds(5, 3), :], SOUTH, (p, north, b)),
        remote(q_hbm.at[:, pl.ds(0, 3), :], field.at[:, pl.ds(16, 3), :], NORTH, (p, south, b)),
        remote(clat_hbm.at[:, pl.ds(0, 1), :], clat.at[:, pl.ds(R, 1), :], NORTH_C, (p, south, b)),
    ]
    for copy in halo:
        copy.start()
    far_first = sorted(range(nz), key=lambda i: -min(i, nz - i))
    for i in far_first:
        peer = at_z(i)
        remote(cm_send.at[peer], cm_recv.at[z], MASSES, (other, peer, b)).start()

    loads[2].wait()
    inside = (lane >= 4) & (lane < 124)
    mass_old = [jnp.zeros((R, C), F32) for _ in range(T)]
    for l in range(L):
        coef = [
            jnp.where(inside, o, 0.0) for o in betas(clon[l], left(clon[l], 1))
        ]
        for t in range(T):
            tile = field[t * L + l, R : 2 * R, :]
            mass_old[t] += mass[l * R : (l + 1) * R, :] * tile
            value = tile
            for k in range(7):
                value -= coef[k] * left(tile, k - 3)
            base[t * L + l] = value

    for copy in halo[:2]:
        copy.wait()
    quarter = lane & 3
    halo_w = jnp.where(b == 0, 0.0, recv_w[0])
    halo_e = jnp.where(b == nlon - 1, 0.0, recv_e[0])
    halo_c = jnp.where(b == nlon - 1, 0.0, recv_e[1])
    c_e_next = jnp.where(quarter == 3, left(halo_c, -3), c_e_next)

    def packed(before, middle, after, coef):
        value = coef[3] * middle
        for k in range(7):
            s = k - 3
            if s < 0:
                cell = jnp.where(quarter < -s, left(before, 4 + s), left(middle, s))
            elif s > 0:
                cell = jnp.where(quarter >= 4 - s, left(after, s - 4), left(middle, s))
            else:
                continue
            value += coef[k] * cell
        return value

    change_w = packed(halo_w, own_w, own_w2, betas(c_w, c_w_next))
    change_e = packed(own_e2, own_e, halo_e, betas(c_e, c_e_next))

    for copy in halo[2:]:
        copy.wait()

    @pl.when(z == 0)
    def _():
        field[:, 5:8, :] = jnp.zeros((F, 3, C), F32)

    @pl.when(z == nz - 1)
    def _():
        field[:, 16:19, :] = jnp.zeros((F, 3, C), F32)
        clat[:, 8:9, :] = jnp.zeros((L, 1, C), F32)

    keep = filled < 0.5
    mass_new = [jnp.zeros((R, C), F32) for _ in range(T)]
    for l in range(L):
        coef = betas(clat[l, 0:8, :], clat[l, 1:9, :])
        kept = jnp.where(keep, mass[l * R : (l + 1) * R, :], 0.0)
        for t in range(T):
            f = t * L + l
            value = base[f]
            value -= jnp.where(lane < 4, left(change_w, 4 * f), 0.0)
            value -= jnp.where(lane >= 124, left(change_e, 4 * f + 4), 0.0)
            for k in range(7):
                value -= coef[k] * field[f, 5 + k : 13 + k, :]
            adv[f * R : (f + 1) * R, :] = value
            mass_new[t] += kept * value

    for r in range(R):
        high, low_part = halves(adv[pl.ds(r, F, stride=R), :])
        at = pl.ds(r * F, F)
        lhs[at, 0:C] = high
        lhs[at, C : 2 * C] = low_part
        lhs[at, 2 * C : 3 * C] = high
    mixed[...] = jnp.dot(lhs[...], colw[...], preferred_element_type=F32)
    for v in range(6):
        total = jnp.zeros((F, C), F32)
        for r in range(R):
            total += roww[r, v : v + 1, :] * mixed[r * F : (r + 1) * F, v * C : (v + 1) * C]
        first, second = total[0 : F // 2, :], total[F // 2 : F, :]
        packet[v] = jnp.where(low16, first, left(second, K))
        packet[v + 6] = jnp.where(low16, left(first, K), second)
    for i in far_first:
        peer = at_z(i)
        remote(packet.at[peer], arrived.at[z], MARGIN, (other, peer, b)).start()

    wait_all(cm_recv, recv_sem.at[MASSES])
    parts = [jnp.zeros((R, C), F32) for _ in range(2)]
    for d in range(12):
        four = cm_recv[d]
        eight = jnp.concatenate([four, left(four, K)], axis=0)
        eight = jnp.where(low, eight, left(eight, K))
        for half in range(2):
            parts[half] += eight * packet[d, half * R : (half + 1) * R, :]
    for half in range(2):
        mass_new[half] += jnp.where(low, parts[half], 0.0)
        mass_new[half + 2] += jnp.where(low, 0.0, parts[half])
    stacked = jnp.concatenate(
        [jnp.sum(m, axis=0, keepdims=True) for m in mass_old + mass_new], axis=0
    )
    sums = jnp.sum(stacked, axis=1, keepdims=True)
    row = jnp.sum(jnp.where(lane == sub[0:R, :], sums, 0.0), axis=0, keepdims=True)

    rows[0] = row
    group = [(other, z, b)]
    group += [(core, z, at_x(i)) for i in range(1, NX) for core in (p, other)]
    for i, device in enumerate(group):
        remote(rows.at[0], sum_x.at[i], SUM_X, device).start()
    wait_all(sum_x, recv_sem.at[SUM_X])
    row = row + jnp.sum(sum_x[...], axis=0)
    rows[1] = row
    for i in range(1, ny):
        remote(rows.at[1], sum_y.at[i - 1], SUM_Y, (p, z, at_y(i))).start()
    wait_all(sum_y, recv_sem.at[SUM_Y])
    row = row + jnp.sum(sum_y[...], axis=0)
    rows[2] = row
    for i in range(1, nz):
        remote(rows.at[2], sum_z.at[i - 1], SUM_Z, (p, at_z(i), b)).start()

    wait_all(arrived, recv_sem.at[MARGIN])
    for v in range(6):
        cols = pl.ds(v * C, C)
        one, two = arrived[v], arrived[v + 6]
        first = jnp.where(low16, one, left(two, K))
        second = jnp.where(low16, left(one, K), two)
        values = jnp.concatenate([first, second], axis=0)
        high = values.astype(BF16).astype(F32)
        low_part = values - high
        for r in range(R):
            at = pl.ds(r * F, F)
            here = live_rows[v] == r
            scat_hi[at, cols] = jnp.where(here, high, 0.0).astype(BF16)
            scat_lo[at, cols] = jnp.where(here, low_part, 0.0).astype(BF16)
    nt = (((1,), (1,)), ((), ()))
    scattered[...] = lax.dot_general(
        scat_hi[...], onehot[...], nt, preferred_element_type=F32
    ) + lax.dot_general(scat_lo[...], onehot[...], nt, preferred_element_type=F32)
    for f in range(F):
        at = pl.ds(f * R, R)
        adv[at, :] = jnp.where(keep, adv[at, :], scattered[pl.ds(f, R, stride=F), :])

    wait_all(sum_z, recv_sem.at[SUM_Z])
    row = row + jnp.sum(sum_z[...], axis=0)
    ratio = row / left(row, 4)
    for t in range(T):
        scale = jnp.broadcast_to(ratio[:, t : t + 1], (R, C))
        for l in range(L):
            f = t * L + l
            out[f] = adv[f * R : (f + 1) * R, :] * scale

    wait_all(cm_send, send_sem.at[MASSES])
    wait_all(packet, send_sem.at[MARGIN])
    wait_all(sum_x, send_sem.at[SUM_X])
    wait_all(sum_y, send_sem.at[SUM_Y])
    wait_all(sum_z, send_sem.at[SUM_Z])


def solution(mesh):
    nz, nlon = mesh.shape["lat"], mesh.shape["lon"]
    ny = nlon // NX

    def body(tracers, courant_lon, courant_lat, cell_mass, donor_cell, donor_frac, target_cell, live_count):
        slots = nz * K
        any_spec = pl.BlockSpec(memory_space=pl.ANY)

        def run(*refs):
            kernel(nz, nlon, *refs)

        result = pl.pallas_call(
            run,
            out_shape=jax.ShapeDtypeStruct((F, R, C), F32),
            in_specs=[any_spec] * 7 + [pl.BlockSpec(memory_space=pltpu.SMEM)],
            out_specs=pl.BlockSpec(memory_space=pltpu.VMEM),
            scratch_shapes=[
                pltpu.VMEM((F, 3 * R, C), F32),
                pltpu.VMEM((L, R, C), F32),
                pltpu.VMEM((L, 2 * R, C), F32),
                pltpu.VMEM((L * R, C), F32),
                pltpu.VMEM((nz, K), jnp.int32),
                pltpu.VMEM((2, nz, K), F32),
                pltpu.VMEM((nz, K), jnp.int32),
                pltpu.VMEM((2, R, C), F32),
                pltpu.VMEM((1, R, C), F32),
                pltpu.VMEM((1, R, C), F32),
                pltpu.VMEM((2, R, C), F32),
                pltpu.VMEM((nz, 4, C), F32),
                pltpu.VMEM((nz, 4, C), F32),
                pltpu.VMEM((nz, 2 * R, C), F32),
                pltpu.VMEM((nz, 2 * R, C), F32),
                pltpu.VMEM((3, 1, C), F32),
                pltpu.VMEM((2 * NX - 1, 1, C), F32),
                pltpu.VMEM((ny - 1, 1, C), F32),
                pltpu.VMEM((nz - 1, 1, C), F32),
                pltpu.VMEM((F, R, C), F32),
                pltpu.VMEM((F * R, C), F32),
                pltpu.VMEM((C, slots), BF16),
                pltpu.VMEM((3 * C, slots), BF16),
                pltpu.VMEM((R, R, C), F32),
                pltpu.VMEM((F * R, 3 * C), BF16),
                pltpu.VMEM((F * R, slots), F32),
                pltpu.VMEM((F * R, slots), BF16),
                pltpu.VMEM((F * R, slots), BF16),
                pltpu.VMEM((2 * R, slots), BF16),
                pltpu.VMEM((F * R, C), F32),
                pltpu.SemaphoreType.DMA((7,)),
                pltpu.SemaphoreType.DMA((10,)),
                pltpu.SemaphoreType.DMA((10,)),
            ],
            compiler_params=pltpu.CompilerParams(collective_id=0, has_side_effects=True),
        )(
            tracers.reshape(F, R, C),
            courant_lon.reshape(L, R, C),
            courant_lat.reshape(L, R, C),
            cell_mass.reshape(L * R, C),
            donor_cell.reshape(nz, K),
            donor_frac.reshape(2, nz, K),
            target_cell.reshape(nz, K),
            live_count.reshape(nz),
        )
        return result.reshape(1, T, L, R, C)

    lon = "lon"
    placed = (
        P("panel", None, None, "lat", lon),
        P("panel", None, "lat", lon),
        P("panel", None, "lat", lon),
        P("panel", None, "lat", lon),
        P("panel", "lat", lon, None, None),
        P(None, "panel", "lat", lon, None, None),
        P("panel", "lat", lon, None, None),
        P("panel", "lat", lon, None),
    )
    return jax.shard_map(
        body,
        mesh=mesh,
        in_specs=placed,
        out_specs=P("panel", None, None, "lat", lon),
        check_vma=False,
    )
```

time: 167 us -> 43.5 us (0.26)
  the two profiles are of different devices: /device:TPU:2 before, /device:TPU:1 now
where the time goes in v1:
time: 43.5 us; the launch traced here: 43.1 us
  Pallas kernels  39.5 us (91%)
  local copies, waits for them, and re-layouts  3.59 us (8%)
    pallas_call x1, Pallas kernels, body(): pl.pallas_call(run, out_shape=jax.ShapeDtypeStruct((F, R, C), F32), in_sp...  39.5 us
    unnamed x7, local copies, waits for them, and re-layouts  2.98 us

profile of v1, /device:TPU:1, one launch (start us, length us, event | category | flops | bytes accessed | tf_op | source)
XLA Modules:
  0.0 43.1 jit_solution(5458572876496235746)
XLA Ops:
  0.0 0.7 %copy.16 = f32[2,1,1,1,12,64]{5,0,4,3,2,1:T(2,128)S(1)} copy(f32[2,1,1,1,12,64]{5,3,4,2,1,0:T(1,128)} %param.13) | data formatting | bytes 12288 | tf_op args[5]
  0.7 0.0 copy-start
  0.7 0.0 copy-start.1
  0.7 0.6 %copy.10.refs_5_ = f32[2,12,64]{2,1,0:T(8,128)} copy(f32[2,12,64]{2,0,1:T(2,128)S(1)} %bitcast.15) | data formatting | bytes 12288 | tf_op jit(solution)/shard_map/reshape | solution.py:443
  1.3 0.1 copy-done
  1.4 0.0 copy-done.1
  1.4 0.6 %copy_bitcast_fusion.1 = (s32[12,64]{1,0:T(8,128)}, s32[12,64]{1,0:T(8,128)}) fusion(s32[1,1,1,12,64]{4,2,3,1,0:T(1,128)S(1)} %copy-done, s32[1,1,1,12,64]{4,2,3,1,0:T(1,128)S(1)} %copy-done.1), kind=kLoop, calls=%fused_computation.1 | loop fusion | bytes 12288
  2.0 39.5 %shard_map.82 = f32[32,8,128]{2,1,0:T(8,128)} custom-call(f32[32,8,128]{2,1,0:T(8,128)} %bitcast.14, f32[8,8,128]{2,1,0:T(8,128)} %bitcast.16, f32[8,8,128]{2,1,0:T(8,128)} %bitcast.17, f32[64,128]{1,0:T(8,128)} %bitcast.18, s32[12,64]{1,0:T(8,128)} %get-tuple-element.6.refs_4_, f32[2,12,64]{2,1,0:T(8,128)} %copy.10.refs_5_, ...), custom_call_target="tpu_custom_call" | custom-call | tf_op jit(solution)/shard_map/pallas_call | solution.py:396
  41.5 1.6 %copy.18 = f32[1,4,8,8,128]{4,3,2,1,0:T(8,128)} copy(f32[1,4,8,8,128]{4,3,2,1,0:T(8,128)} %bitcast.13) | data formatting | bytes 262144
Async XLA Ops:
  0.7 0.7 %copy-start = (s32[1,1,1,12,64]{4,2,3,1,0:T(1,128)S(1)}, s32[1,1,1,12,64]{4,2,3,1,0:T(1,128)}, u32[]{:S(2)}) copy-start(s32[1,1,1,12,64]{4,2,3,1,0:T(1,128)} %param.14) | copy-start | bytes 9220
  0.7 0.7 %copy-start.1 = (s32[1,1,1,12,64]{4,2,3,1,0:T(1,128)S(1)}, s32[1,1,1,12,64]{4,2,3,1,0:T(1,128)}, u32[]{:S(2)}) copy-start(s32[1,1,1,12,64]{4,2,3,1,0:T(1,128)} %param.12) | copy-start | bytes 9220

commit v2 on v1

--- a/solution.py
+++ b/solution.py
@@ -80,8 +80,8 @@
     pltpu.make_async_copy(ref, ref, sem).wait()
 
 
-def kernel(nz, nlon, q_hbm, clon_hbm, clat_hbm, mass_hbm, donor_hbm, frac_hbm, target_hbm, live,
-           out, field, clon, clat, mass, donor, frac, target, send_w, send_e, recv_w, recv_e,
+def kernel(nz, nlon, q_hbm, clon_hbm, clat_hbm, mass_hbm, donor_hbm, frac_hbm, target_hbm, live_hbm,
+           out, scale_out, field, clon, clat, mass, donor, frac, target, live, send_w, send_e, recv_w, recv_e,
            cm_send, cm_recv, packet, arrived, rows, sum_x, sum_y, sum_z, base, adv, onehot, colw,
            roww, lhs, mixed, scat_hi, scat_lo, rowmask, scattered, local_sem, send_sem, recv_sem):
     p = lax.axis_index("panel")
@@ -111,6 +111,7 @@
         pltpu.make_async_copy(donor_hbm, donor, local_sem.at[4]),
         pltpu.make_async_copy(frac_hbm, frac, local_sem.at[5]),
         pltpu.make_async_copy(target_hbm, target, local_sem.at[6]),
+        pltpu.make_async_copy(live_hbm, live, local_sem.at[7]),
     ]
     barrier = pltpu.get_barrier_semaphore()
     partners = [(other, at_z(i), b) for i in range(nz)] + [(p, at_z(i), b) for i in range(1, nz)]
@@ -130,7 +131,14 @@
     low, low16 = lane < K, lane16 < K
 
     loads[6].wait()
-    spots = jnp.concatenate([target[0:6, :], target[6:12, :]], axis=1)
+    loads[7].wait()
+
+    def slots(read):
+        return jnp.concatenate(
+            [jnp.concatenate([read(v), read(v + 6)], axis=1) for v in range(6)], axis=0
+        )
+
+    spots = slots(lambda d: target[d])
     spot_col = spots & (C - 1)
     spot_row = spots >> 7
     live_rows = []
@@ -160,6 +168,33 @@
         turned = left(total, K)
         cm_send[v] = jnp.where(low, total, pltpu.roll(turned, 4, 0))[0:4, :]
         cm_send[v + 6] = jnp.where(low, turned, pltpu.roll(total, 4, 0))[0:4, :]
+
+    pl.semaphore_wait(barrier, len(partners))
+
+    def remote(src, dst, which, device):
+        return pltpu.make_async_remote_copy(
+            src_ref=src,
+            dst_ref=dst,
+            send_sem=send_sem.at[which],
+            recv_sem=recv_sem.at[which],
+            device_id=device,
+            device_id_type=MESH,
+        )
+
+    far_first = sorted(range(nz), key=lambda i: -min(i, nz - i))
+    for i in far_first:
+        peer = at_z(i)
+        remote(cm_send.at[peer], cm_recv.at[z], MASSES, (other, peer, b)).start()
+
+    halo = [
+        remote(send_w, recv_e, EAST, (p, z, west)),
+        remote(send_e, recv_w, WEST, (p, z, east)),
+        remote(q_hbm.at[:, pl.ds(5, 3), :], field.at[:, pl.ds(5, 3), :], SOUTH, (p, north, b)),
+        remote(q_hbm.at[:, pl.ds(0, 3), :], field.at[:, pl.ds(16, 3), :], NORTH, (p, south, b)),
+        remote(clat_hbm.at[:, pl.ds(0, 1), :], clat.at[:, pl.ds(R, 1), :], NORTH_C, (p, south, b)),
+    ]
+    for copy in halo[2:]:
+        copy.start()
 
     loads[0].wait()
     loads[1].wait()
@@ -181,14 +216,16 @@
     send_w[0] = own_w
     send_w[1] = c_w
     send_e[0] = own_e
+    for copy in halo[:2]:
+        copy.start()
 
     loads[4].wait()
     loads[5].wait()
-    cells = jnp.concatenate([donor[0:6, :], donor[6:12, :]], axis=1)
+    cells = slots(lambda d: donor[d])
     start_col = cells & (C - 1)
     start_row = cells >> 7
-    row_weights = cubic(jnp.concatenate([frac[0, 0:6, :], frac[0, 6:12, :]], axis=1))
-    col_weights = cubic(jnp.concatenate([frac[1, 0:6, :], frac[1, 6:12, :]], axis=1))
+    row_weights = cubic(slots(lambda d: frac[0, d]))
+    col_weights = cubic(slots(lambda d: frac[1, d]))
     for r in range(R):
         roww[r, 0:6, :] = pick(r - start_row, row_weights)
     for v in range(6):
@@ -200,32 +237,6 @@
         colw[0:C, cols] = high
         colw[C : 2 * C, cols] = high
         colw[2 * C : 3 * C, cols] = low_part
-
-    pl.semaphore_wait(barrier, len(partners))
-
-    def remote(src, dst, which, device):
-        return pltpu.make_async_remote_copy(
-            src_ref=src,
-            dst_ref=dst,
-            send_sem=send_sem.at[which],
-            recv_sem=recv_sem.at[which],
-            device_id=device,
-            device_id_type=MESH,
-        )
-
-    halo = [
-        remote(send_w, recv_e, EAST, (p, z, west)),
-        remote(send_e, recv_w, WEST, (p, z, east)),
-        remote(q_hbm.at[:, pl.ds(5, 3), :], field.at[:, pl.ds(5, 3), :], SOUTH, (p, north, b)),
-        remote(q_hbm.at[:, pl.ds(0, 3), :], field.at[:, pl.ds(16, 3), :], NORTH, (p, south, b)),
-        remote(clat_hbm.at[:, pl.ds(0, 1), :], clat.at[:, pl.ds(R, 1), :], NORTH_C, (p, south, b)),
-    ]
-    for copy in halo:
-        copy.start()
-    far_first = sorted(range(nz), key=lambda i: -min(i, nz - i))
-    for i in far_first:
-        peer = at_z(i)
-        remote(cm_send.at[peer], cm_recv.at[z], MASSES, (other, peer, b)).start()
 
     loads[2].wait()
     inside = (lane >= 4) & (lane < 124)
@@ -364,16 +375,13 @@
     ) + lax.dot_general(scat_lo[...], onehot[...], nt, preferred_element_type=F32)
     for f in range(F):
         at = pl.ds(f * R, R)
-        adv[at, :] = jnp.where(keep, adv[at, :], scattered[pl.ds(f, R, stride=F), :])
+        out[f] = jnp.where(keep, adv[at, :], scattered[pl.ds(f, R, stride=F), :])
 
     wait_all(sum_z, recv_sem.at[SUM_Z])
     row = row + jnp.sum(sum_z[...], axis=0)
     ratio = row / left(row, 4)
     for t in range(T):
-        scale = jnp.broadcast_to(ratio[:, t : t + 1], (R, C))
-        for l in range(L):
-            f = t * L + l
-            out[f] = adv[f * R : (f + 1) * R, :] * scale
+        scale_out[t] = jnp.broadcast_to(ratio[:, t : t + 1], (R, C))
 
     wait_all(cm_send, send_sem.at[MASSES])
     wait_all(packet, send_sem.at[MARGIN])
@@ -388,24 +396,29 @@
 
     def body(tracers, courant_lon, courant_lat, cell_mass, donor_cell, donor_frac, target_cell, live_count):
         slots = nz * K
-        any_spec = pl.BlockSpec(memory_space=pl.ANY)
+        hbm_spec = pl.BlockSpec(memory_space=pltpu.HBM)
+        vmem_spec = pl.BlockSpec(memory_space=pltpu.VMEM)
 
         def run(*refs):
             kernel(nz, nlon, *refs)
 
-        result = pl.pallas_call(
+        merged, scale = pl.pallas_call(
             run,
-            out_shape=jax.ShapeDtypeStruct((F, R, C), F32),
-            in_specs=[any_spec] * 7 + [pl.BlockSpec(memory_space=pltpu.SMEM)],
-            out_specs=pl.BlockSpec(memory_space=pltpu.VMEM),
+            out_shape=(
+                pltpu.VMEM((F, R, C), F32),
+                pltpu.VMEM((T, R, C), F32),
+            ),
+            in_specs=[hbm_spec] * 8,
+            out_specs=(vmem_spec, vmem_spec),
             scratch_shapes=[
                 pltpu.VMEM((F, 3 * R, C), F32),
                 pltpu.VMEM((L, R, C), F32),
                 pltpu.VMEM((L, 2 * R, C), F32),
                 pltpu.VMEM((L * R, C), F32),
-                pltpu.VMEM((nz, K), jnp.int32),
-                pltpu.VMEM((2, nz, K), F32),
-                pltpu.VMEM((nz, K), jnp.int32),
+                pltpu.VMEM((nz, 1, K), jnp.int32),
+                pltpu.VMEM((2, nz, 1, K), F32),
+                pltpu.VMEM((nz, 1, K), jnp.int32),
+                pltpu.SMEM((nz,), jnp.int32),
                 pltpu.VMEM((2, R, C), F32),
                 pltpu.VMEM((1, R, C), F32),
                 pltpu.VMEM((1, R, C), F32),
@@ -429,7 +442,7 @@
                 pltpu.VMEM((F * R, slots), BF16),
                 pltpu.VMEM((2 * R, slots), BF16),
                 pltpu.VMEM((F * R, C), F32),
-                pltpu.SemaphoreType.DMA((7,)),
+                pltpu.SemaphoreType.DMA((8,)),
                 pltpu.SemaphoreType.DMA((10,)),
                 pltpu.SemaphoreType.DMA((10,)),
             ],
@@ -439,12 +452,12 @@
             courant_lon.reshape(L, R, C),
             courant_lat.reshape(L, R, C),
             cell_mass.reshape(L * R, C),
-            donor_cell.reshape(nz, K),
-            donor_frac.reshape(2, nz, K),
-            target_cell.reshape(nz, K),
+            donor_cell.reshape(nz, 1, K),
+            donor_frac.reshape(2, nz, 1, K),
+            target_cell.reshape(nz, 1, K),
             live_count.reshape(nz),
         )
-        return result.reshape(1, T, L, R, C)
+        return merged.reshape(1, T, L, R, C) * scale.reshape(1, T, 1, R, C)
 
     lon = "lon"
     placed = (

time: 43.5 us -> 39 us (0.90)
  local copies, waits for them, and re-layouts: 3.59 us -> 0 us
  Pallas kernels: 39.5 us -> 38.1 us
  other arithmetic: 0 us -> 0.67 us
    unnamed x7 -> x0, local copies, waits for them, and re-layouts: 2.98 us -> none
    pallas_call x1, Pallas kernels: 39.5 us -> 38.1 us  [body(): pl.pallas_call(run, out_shape=(pltpu.VMEM((F, R, C), F32), pltpu.VMEM((T,...]
    mul x0 -> x1, other arithmetic: none -> 0.67 us  [body(): return merged.reshape(1, T, L, R, C) * scale.reshape(1, T, 1, R, C)]
    reshape x1 -> x0, local copies, waits for them, and re-layouts: 0.61 us -> none  [body(): donor_frac.reshape(2, nz, K)]
where the time goes in v2:
time: 39 us; the launch traced here: 38.8 us
  Pallas kernels  38.1 us (98%)
  other arithmetic  0.67 us (2%)
    pallas_call x1, Pallas kernels, body(): pl.pallas_call(run, out_shape=(pltpu.VMEM((F, R, C), F32), pltpu.VMEM((T,...  38.1 us

profile of v2, /device:TPU:1, one launch (start us, length us, event | category | flops | bytes accessed | tf_op | source)
XLA Modules:
  0.0 38.8 jit_solution(11624802474840675097)
XLA Ops:
  0.0 38.1 %shard_map.82 = (f32[32,8,128]{2,1,0:T(8,128)S(1)}, f32[4,8,128]{2,1,0:T(8,128)S(1)}) custom-call(f32[32,8,128]{2,1,0:T(8,128)} %bitcast.10, f32[8,8,128]{2,1,0:T(8,128)} %bitcast.11, f32[8,8,128]{2,1,0:T(8,128)} %bitcast.12, f32[64,128]{1,0:T(8,128)} %bitcast.13, s32[12,1,64]{2,1,0:T(1,128)} %bitcast.15, f32[2,12,1,64]{3,2,1,0:T(1,128)} %bitcast.14, ...), custom_call_target="tpu_custom_call" | custom-call | tf_op jit(solution)/shard_map/pallas_call | solution.py:405
  38.2 0.7 %broadcast_multiply_fusion = f32[1,4,8,8,128]{4,3,2,1,0:T(8,128)} fusion(f32[1,4,8,8,128]{4,3,2,1,0:T(8,128)S(1)} %bitcast.9, f32[4,8,128]{2,1,0:T(8,128)S(1)} %get-tuple-element.8), kind=kLoop, calls=%fused_computation | loop fusion | flops 32768 | bytes 278528 | tf_op jit(solution)/shard_map/mul | solution.py:460

commit v3 on v2

--- a/solution.py
+++ b/solution.py
@@ -16,7 +16,7 @@
 C = 128
 K = 64
 NX = 4
-WEST, EAST, SOUTH, NORTH, NORTH_C, MASSES, MARGIN, SUM_X, SUM_Y, SUM_Z = range(10)
+WEST, EAST, SOUTH, NORTH, NORTH_C, MASSES, MARGIN, SUM_XY, SUM_Z = range(9)
 
 
 def left(x, by):
@@ -82,8 +82,8 @@
 
 def kernel(nz, nlon, q_hbm, clon_hbm, clat_hbm, mass_hbm, donor_hbm, frac_hbm, target_hbm, live_hbm,
            out, scale_out, field, clon, clat, mass, donor, frac, target, live, send_w, send_e, recv_w, recv_e,
-           cm_send, cm_recv, packet, arrived, rows, sum_x, sum_y, sum_z, base, adv, onehot, colw,
-           roww, lhs, mixed, scat_hi, scat_lo, rowmask, scattered, local_sem, send_sem, recv_sem):
+           cm_send, cm_recv, relayed, packet, arrived, rows, sum_xy, sum_z, base, adv, onehot, colw,
+           roww, lhs, mixed, scat_hi, scat_lo, rowmask, scattered, local_sem, send_sem, recv_sem, relay_send, relay_recv, plane_sem):
     p = lax.axis_index("panel")
     z = lax.axis_index("lat")
     b = lax.axis_index("lon")
@@ -93,12 +93,6 @@
 
     def at_z(step):
         return lax.rem(z + step, nz)
-
-    def at_x(step):
-        return y * NX + lax.rem(x + step, NX)
-
-    def at_y(step):
-        return lax.rem(y + step, ny) * NX + x
 
     west, east = lax.rem(b + nlon - 1, nlon), lax.rem(b + 1, nlon)
     south, north = at_z(nz - 1), at_z(1)
@@ -114,14 +108,36 @@
         pltpu.make_async_copy(live_hbm, live, local_sem.at[7]),
     ]
     barrier = pltpu.get_barrier_semaphore()
-    partners = [(other, at_z(i), b) for i in range(nz)] + [(p, at_z(i), b) for i in range(1, nz)]
-    partners += [(p, z, west), (p, z, east)]
-    partners += [(core, z, at_x(i)) for i in range(1, NX) for core in (p, other)]
-    partners += [(p, z, at_y(i)) for i in range(1, ny)]
-    for partner in partners:
-        pl.semaphore_signal(barrier, inc=1, device_id=partner, device_id_type=MESH)
-    for load in loads:
+    far_first = sorted(range(nz), key=lambda i: -min(i, nz - i))
+    plane = [(i, j) for i in range(ny) for j in range(NX) if i + j > 0]
+    plane.sort(key=lambda ij: -min(ij[0], ny - ij[0]) - min(ij[1], NX - ij[1]))
+
+    def at_plane(i, j):
+        return lax.rem(y + i, ny) * NX + lax.rem(x + j, NX)
+
+    def signal(sem, device):
+        pl.semaphore_signal(sem, inc=1, device_id=device, device_id_type=MESH)
+
+    far = sorted(range(4, nz - 3), key=lambda i: -min(i, nz - i))
+    far_low = min(far)
+    close = [i for i in far_first if i not in far]
+    across = [at_plane(0, j) for j in range(1, NX)]
+    along = [at_plane(2, 0), at_plane(ny - 2, 0)]
+    greeted = [(core, at_z(i), b) for i in close if i for core in (other, p)] + [(other, z, b)]
+    greeted += [(p, z, c) for c in along + across + [at_plane(1, 0), at_plane(ny - 1, 0), west, east]]
+    lower = sum(lax.div(z + i, nz) for i in far)
+
+    for load in (loads[6], loads[7], loads[3], *loads[:3], *loads[4:6]):
         load.start()
+    for i in far:
+
+        @pl.when(z + i < nz)
+        def _():
+            for core in (other, p):
+                signal(barrier, (core, z + i, b))
+
+    for device in greeted:
+        signal(barrier, device)
 
     lane = lax.broadcasted_iota(jnp.int32, (R, C), 1)
     lane16 = lax.broadcasted_iota(jnp.int32, (2 * R, C), 1)
@@ -169,7 +185,7 @@
         cm_send[v] = jnp.where(low, total, pltpu.roll(turned, 4, 0))[0:4, :]
         cm_send[v + 6] = jnp.where(low, turned, pltpu.roll(total, 4, 0))[0:4, :]
 
-    pl.semaphore_wait(barrier, len(partners))
+    pl.semaphore_wait(barrier, len(greeted) + 2 * lower)
 
     def remote(src, dst, which, device):
         return pltpu.make_async_remote_copy(
@@ -181,10 +197,35 @@
             device_id_type=MESH,
         )
 
-    far_first = sorted(range(nz), key=lambda i: -min(i, nz - i))
-    for i in far_first:
-        peer = at_z(i)
+    def send_masses(peer):
         remote(cm_send.at[peer], cm_recv.at[z], MASSES, (other, peer, b)).start()
+
+    def relay(src, dst, i, device):
+        return pltpu.make_async_remote_copy(
+            src_ref=src,
+            dst_ref=dst,
+            send_sem=relay_send.at[i - far_low],
+            recv_sem=relay_recv.at[i - far_low],
+            device_id=device,
+            device_id_type=MESH,
+        )
+
+    def relay_step(i):
+        return 3 if 2 * i <= nz else nz - 3
+
+    for i in far:
+
+        @pl.when(z + i >= nz)
+        def _():
+            send_masses(z + i - nz)
+
+        @pl.when(z + i < nz)
+        def _():
+            via = (other, at_z(relay_step(i)), b)
+            relay(cm_send.at[z + i], relayed.at[i - far_low], i, via).start()
+
+    for i in close:
+        send_masses(at_z(i))
 
     halo = [
         remote(send_w, recv_e, EAST, (p, z, west)),
@@ -218,6 +259,8 @@
     send_e[0] = own_e
     for copy in halo[:2]:
         copy.start()
+    for c in along:
+        signal(plane_sem.at[0], (p, z, c))
 
     loads[4].wait()
     loads[5].wait()
@@ -253,6 +296,18 @@
                 value -= coef[k] * left(tile, k - 3)
             base[t * L + l] = value
 
+    pl.semaphore_wait(plane_sem.at[0], 2)
+    for c in across:
+        signal(plane_sem.at[1], (p, z, c))
+    for i in far:
+        origin = at_z(nz - relay_step(i))
+
+        @pl.when(origin + i < nz)
+        def _():
+            slot = relayed.at[i - far_low]
+            pltpu.make_async_copy(slot, slot, relay_recv.at[i - far_low]).wait()
+            remote(slot, cm_recv.at[origin], MASSES, (p, origin + i, b)).start()
+
     for copy in halo[:2]:
         copy.wait()
     quarter = lane & 3
@@ -318,11 +373,11 @@
         first, second = total[0 : F // 2, :], total[F // 2 : F, :]
         packet[v] = jnp.where(low16, first, left(second, K))
         packet[v + 6] = jnp.where(low16, left(first, K), second)
+
+    wait_all(cm_recv, recv_sem.at[MASSES])
     for i in far_first:
         peer = at_z(i)
         remote(packet.at[peer], arrived.at[z], MARGIN, (other, peer, b)).start()
-
-    wait_all(cm_recv, recv_sem.at[MASSES])
     parts = [jnp.zeros((R, C), F32) for _ in range(2)]
     for d in range(12):
         four = cm_recv[d]
@@ -339,21 +394,16 @@
     sums = jnp.sum(stacked, axis=1, keepdims=True)
     row = jnp.sum(jnp.where(lane == sub[0:R, :], sums, 0.0), axis=0, keepdims=True)
 
-    rows[0] = row
-    group = [(other, z, b)]
-    group += [(core, z, at_x(i)) for i in range(1, NX) for core in (p, other)]
-    for i, device in enumerate(group):
-        remote(rows.at[0], sum_x.at[i], SUM_X, device).start()
-    wait_all(sum_x, recv_sem.at[SUM_X])
-    row = row + jnp.sum(sum_x[...], axis=0)
-    rows[1] = row
-    for i in range(1, ny):
-        remote(rows.at[1], sum_y.at[i - 1], SUM_Y, (p, z, at_y(i))).start()
-    wait_all(sum_y, recv_sem.at[SUM_Y])
-    row = row + jnp.sum(sum_y[...], axis=0)
-    rows[2] = row
-    for i in range(1, nz):
-        remote(rows.at[2], sum_z.at[i - 1], SUM_Z, (p, at_z(i), b)).start()
+    rows[0:1, :] = row
+    pl.semaphore_wait(plane_sem.at[1], len(across))
+    for n, (i, j) in enumerate(plane):
+        remote(rows.at[pl.ds(0, 1), :], sum_xy.at[pl.ds(n, 1), :], SUM_XY, (p, z, at_plane(i, j))).start()
+    wait_all(sum_xy, recv_sem.at[SUM_XY])
+    row = row + jnp.sum(sum_xy[...], axis=0, keepdims=True)
+    rows[1:2, :] = row
+    line = [(core, i) for i in far_first if i > 0 for core in (p, other)] + [(other, 0)]
+    for n, (core, i) in enumerate(line):
+        remote(rows.at[pl.ds(1, 1), :], sum_z.at[pl.ds(n, 1), :], SUM_Z, (core, at_z(i), b)).start()
 
     wait_all(arrived, recv_sem.at[MARGIN])
     for v in range(6):
@@ -378,15 +428,29 @@
         out[f] = jnp.where(keep, adv[at, :], scattered[pl.ds(f, R, stride=F), :])
 
     wait_all(sum_z, recv_sem.at[SUM_Z])
-    row = row + jnp.sum(sum_z[...], axis=0)
+    row = row + jnp.sum(sum_z[...], axis=0, keepdims=True)
     ratio = row / left(row, 4)
     for t in range(T):
         scale_out[t] = jnp.broadcast_to(ratio[:, t : t + 1], (R, C))
 
-    wait_all(cm_send, send_sem.at[MASSES])
+    for i in close:
+        wait_all(cm_send.at[0], send_sem.at[MASSES])
+    for i in far:
+
+        @pl.when(z + i >= nz)
+        def _():
+            wait_all(cm_send.at[0], send_sem.at[MASSES])
+
+        @pl.when(z + i < nz)
+        def _():
+            wait_all(cm_send.at[0], relay_send.at[i - far_low])
+
+        @pl.when(at_z(nz - relay_step(i)) + i < nz)
+        def _():
+            wait_all(cm_send.at[0], send_sem.at[MASSES])
+
     wait_all(packet, send_sem.at[MARGIN])
-    wait_all(sum_x, send_sem.at[SUM_X])
-    wait_all(sum_y, send_sem.at[SUM_Y])
+    wait_all(sum_xy, send_sem.at[SUM_XY])
     wait_all(sum_z, send_sem.at[SUM_Z])
 
 
@@ -425,12 +489,12 @@
                 pltpu.VMEM((2, R, C), F32),
                 pltpu.VMEM((nz, 4, C), F32),
                 pltpu.VMEM((nz, 4, C), F32),
+                pltpu.VMEM((nz - 7, 4, C), F32),
                 pltpu.VMEM((nz, 2 * R, C), F32),
                 pltpu.VMEM((nz, 2 * R, C), F32),
-                pltpu.VMEM((3, 1, C), F32),
-                pltpu.VMEM((2 * NX - 1, 1, C), F32),
-                pltpu.VMEM((ny - 1, 1, C), F32),
-                pltpu.VMEM((nz - 1, 1, C), F32),
+                pltpu.VMEM((2, C), F32),
+                pltpu.VMEM((nlon - 1, C), F32),
+                pltpu.VMEM((2 * nz - 1, C), F32),
                 pltpu.VMEM((F, R, C), F32),
                 pltpu.VMEM((F * R, C), F32),
                 pltpu.VMEM((C, slots), BF16),
@@ -443,8 +507,11 @@
                 pltpu.VMEM((2 * R, slots), BF16),
                 pltpu.VMEM((F * R, C), F32),
                 pltpu.SemaphoreType.DMA((8,)),
-                pltpu.SemaphoreType.DMA((10,)),
-                pltpu.SemaphoreType.DMA((10,)),
+                pltpu.SemaphoreType.DMA((9,)),
+                pltpu.SemaphoreType.DMA((9,)),
+                pltpu.SemaphoreType.DMA((nz - 7,)),
+                pltpu.SemaphoreType.DMA((nz - 7,)),
+                pltpu.SemaphoreType.REGULAR((2,)),
             ],
             compiler_params=pltpu.CompilerParams(collective_id=0, has_side_effects=True),
         )(

time: 39 us -> 39.1 us (level)
  no operation moved by 1% of the time
where the time goes in v3:
time: 39.1 us; the launch traced here: 38.9 us
  Pallas kernels  38.2 us (98%)
  other arithmetic  0.67 us (2%)
    pallas_call x1, Pallas kernels, body(): pl.pallas_call(run, out_shape=(pltpu.VMEM((F, R, C), F32), pltpu.VMEM((T,...  38.2 us

profile of v3, /device:TPU:1, one launch (start us, length us, event | category | flops | bytes accessed | tf_op | source)
XLA Modules:
  0.0 38.9 jit_solution(15481460819116981814)
XLA Ops:
  0.0 38.2 %shard_map.82 = (f32[32,8,128]{2,1,0:T(8,128)S(1)}, f32[4,8,128]{2,1,0:T(8,128)S(1)}) custom-call(f32[32,8,128]{2,1,0:T(8,128)} %bitcast.10, f32[8,8,128]{2,1,0:T(8,128)} %bitcast.11, f32[8,8,128]{2,1,0:T(8,128)} %bitcast.12, f32[64,128]{1,0:T(8,128)} %bitcast.13, s32[12,1,64]{2,1,0:T(1,128)} %bitcast.15, f32[2,12,1,64]{3,2,1,0:T(1,128)} %bitcast.14, ...), custom_call_target="tpu_custom_call" | custom-call | tf_op jit(solution)/shard_map/pallas_call | solution.py:469
  38.2 0.7 %broadcast_multiply_fusion = f32[1,4,8,8,128]{4,3,2,1,0:T(8,128)} fusion(f32[1,4,8,8,128]{4,3,2,1,0:T(8,128)S(1)} %bitcast.9, f32[4,8,128]{2,1,0:T(8,128)S(1)} %get-tuple-element.8), kind=kLoop, calls=%fused_computation | loop fusion | flops 32768 | bytes 278528 | tf_op jit(solution)/shard_map/mul | solution.py:527

commit v4 on v2

--- a/solution.py
+++ b/solution.py
@@ -16,7 +16,7 @@
 C = 128
 K = 64
 NX = 4
-WEST, EAST, SOUTH, NORTH, NORTH_C, MASSES, MARGIN, SUM_X, SUM_Y, SUM_Z = range(10)
+WEST, EAST, SOUTH, NORTH, NORTH_C, MASSES, MARGIN, SUM_XY, SUM_Z = range(9)
 
 
 def left(x, by):
@@ -82,7 +82,7 @@
 
 def kernel(nz, nlon, q_hbm, clon_hbm, clat_hbm, mass_hbm, donor_hbm, frac_hbm, target_hbm, live_hbm,
            out, scale_out, field, clon, clat, mass, donor, frac, target, live, send_w, send_e, recv_w, recv_e,
-           cm_send, cm_recv, packet, arrived, rows, sum_x, sum_y, sum_z, base, adv, onehot, colw,
+           cm_send, cm_recv, packet, arrived, rows, sum_xy, sum_z, mass_old, base, latw, adv, onehot, colw,
            roww, lhs, mixed, scat_hi, scat_lo, rowmask, scattered, local_sem, send_sem, recv_sem):
     p = lax.axis_index("panel")
     z = lax.axis_index("lat")
@@ -93,12 +93,6 @@
 
     def at_z(step):
         return lax.rem(z + step, nz)
-
-    def at_x(step):
-        return y * NX + lax.rem(x + step, NX)
-
-    def at_y(step):
-        return lax.rem(y + step, ny) * NX + x
 
     west, east = lax.rem(b + nlon - 1, nlon), lax.rem(b + 1, nlon)
     south, north = at_z(nz - 1), at_z(1)
@@ -114,14 +108,19 @@
         pltpu.make_async_copy(live_hbm, live, local_sem.at[7]),
     ]
     barrier = pltpu.get_barrier_semaphore()
-    partners = [(other, at_z(i), b) for i in range(nz)] + [(p, at_z(i), b) for i in range(1, nz)]
-    partners += [(p, z, west), (p, z, east)]
-    partners += [(core, z, at_x(i)) for i in range(1, NX) for core in (p, other)]
-    partners += [(p, z, at_y(i)) for i in range(1, ny)]
+    far_first = sorted(range(nz), key=lambda i: -min(i, nz - i))
+    partners = [(core, at_z(i), b) for i in far_first[:-1] for core in (other, p)] + [(other, z, b)]
+    plane = [(i, j) for i in range(ny) for j in range(NX) if i + j > 0]
+    plane.sort(key=lambda ij: -min(ij[0], ny - ij[0]) - min(ij[1], NX - ij[1]))
+
+    def at_plane(i, j):
+        return lax.rem(y + i, ny) * NX + lax.rem(x + j, NX)
+
+    partners += [(p, z, at_plane(i, j)) for i, j in plane]
+    for load in (loads[6], loads[7], loads[3], *loads[:3], *loads[4:6]):
+        load.start()
     for partner in partners:
         pl.semaphore_signal(barrier, inc=1, device_id=partner, device_id_type=MESH)
-    for load in loads:
-        load.start()
 
     lane = lax.broadcasted_iota(jnp.int32, (R, C), 1)
     lane16 = lax.broadcasted_iota(jnp.int32, (2 * R, C), 1)
@@ -169,35 +168,9 @@
         cm_send[v] = jnp.where(low, total, pltpu.roll(turned, 4, 0))[0:4, :]
         cm_send[v + 6] = jnp.where(low, turned, pltpu.roll(total, 4, 0))[0:4, :]
 
-    pl.semaphore_wait(barrier, len(partners))
-
-    def remote(src, dst, which, device):
-        return pltpu.make_async_remote_copy(
-            src_ref=src,
-            dst_ref=dst,
-            send_sem=send_sem.at[which],
-            recv_sem=recv_sem.at[which],
-            device_id=device,
-            device_id_type=MESH,
-        )
-
-    far_first = sorted(range(nz), key=lambda i: -min(i, nz - i))
-    for i in far_first:
-        peer = at_z(i)
-        remote(cm_send.at[peer], cm_recv.at[z], MASSES, (other, peer, b)).start()
-
-    halo = [
-        remote(send_w, recv_e, EAST, (p, z, west)),
-        remote(send_e, recv_w, WEST, (p, z, east)),
-        remote(q_hbm.at[:, pl.ds(5, 3), :], field.at[:, pl.ds(5, 3), :], SOUTH, (p, north, b)),
-        remote(q_hbm.at[:, pl.ds(0, 3), :], field.at[:, pl.ds(16, 3), :], NORTH, (p, south, b)),
-        remote(clat_hbm.at[:, pl.ds(0, 1), :], clat.at[:, pl.ds(R, 1), :], NORTH_C, (p, south, b)),
-    ]
-    for copy in halo[2:]:
-        copy.start()
-
     loads[0].wait()
     loads[1].wait()
+    loads[2].wait()
     own = [jnp.zeros((R, C), F32) for _ in range(4)]
     firsts = (0, 4, 124, 120)
     for f in range(F):
@@ -216,43 +189,76 @@
     send_w[0] = own_w
     send_w[1] = c_w
     send_e[0] = own_e
+    def prepare():
+        loads[4].wait()
+        loads[5].wait()
+        cells = slots(lambda d: donor[d])
+        start_col = cells & (C - 1)
+        start_row = cells >> 7
+        row_weights = cubic(slots(lambda d: frac[0, d]))
+        col_weights = cubic(slots(lambda d: frac[1, d]))
+        for r in range(R):
+            roww[r, 0:6, :] = pick(r - start_row, row_weights)
+        for v in range(6):
+            cols = pl.ds(v * C, C)
+            weights = pick(
+                column - start_col[v : v + 1, :], [w[v : v + 1, :] for w in col_weights]
+            )
+            high, low_part = halves(weights)
+            colw[0:C, cols] = high
+            colw[C : 2 * C, cols] = high
+            colw[2 * C : 3 * C, cols] = low_part
+
+        inside = (lane >= 4) & (lane < 124)
+        old = [jnp.zeros((R, C), F32) for _ in range(T)]
+        for l in range(L):
+            coef = [
+                jnp.where(inside, o, 0.0) for o in betas(clon[l], left(clon[l], 1))
+            ]
+            for t in range(T):
+                tile = field[t * L + l, R : 2 * R, :]
+                old[t] += mass[l * R : (l + 1) * R, :] * tile
+                value = tile
+                for k in range(7):
+                    value -= coef[k] * left(tile, k - 3)
+                base[t * L + l] = value
+        for t in range(T):
+            mass_old[t] = old[t]
+
+    late = z >= nz - 4
+    pl.when(jnp.logical_not(late))(prepare)
+    pl.semaphore_wait(barrier, len(partners))
+
+    def remote(src, dst, which, device):
+        return pltpu.make_async_remote_copy(
+            src_ref=src,
+            dst_ref=dst,
+            send_sem=send_sem.at[which],
+            recv_sem=recv_sem.at[which],
+            device_id=device,
+            device_id_type=MESH,
+        )
+
+    far_first = sorted(range(nz), key=lambda i: -min(i, nz - i))
+    halo = [
+        remote(send_w, recv_e, EAST, (p, z, west)),
+        remote(send_e, recv_w, WEST, (p, z, east)),
+        remote(field.at[:, pl.ds(13, 3), :], field.at[:, pl.ds(5, 3), :], SOUTH, (p, north, b)),
+        remote(field.at[:, pl.ds(8, 3), :], field.at[:, pl.ds(16, 3), :], NORTH, (p, south, b)),
+        remote(clat.at[:, pl.ds(0, 1), :], clat.at[:, pl.ds(R, 1), :], NORTH_C, (p, south, b)),
+    ]
     for copy in halo[:2]:
         copy.start()
-
-    loads[4].wait()
-    loads[5].wait()
-    cells = slots(lambda d: donor[d])
-    start_col = cells & (C - 1)
-    start_row = cells >> 7
-    row_weights = cubic(slots(lambda d: frac[0, d]))
-    col_weights = cubic(slots(lambda d: frac[1, d]))
-    for r in range(R):
-        roww[r, 0:6, :] = pick(r - start_row, row_weights)
-    for v in range(6):
-        cols = pl.ds(v * C, C)
-        weights = pick(
-            column - start_col[v : v + 1, :], [w[v : v + 1, :] for w in col_weights]
-        )
-        high, low_part = halves(weights)
-        colw[0:C, cols] = high
-        colw[C : 2 * C, cols] = high
-        colw[2 * C : 3 * C, cols] = low_part
-
-    loads[2].wait()
-    inside = (lane >= 4) & (lane < 124)
-    mass_old = [jnp.zeros((R, C), F32) for _ in range(T)]
-    for l in range(L):
-        coef = [
-            jnp.where(inside, o, 0.0) for o in betas(clon[l], left(clon[l], 1))
-        ]
-        for t in range(T):
-            tile = field[t * L + l, R : 2 * R, :]
-            mass_old[t] += mass[l * R : (l + 1) * R, :] * tile
-            value = tile
-            for k in range(7):
-                value -= coef[k] * left(tile, k - 3)
-            base[t * L + l] = value
-
+    for i in far_first[:5]:
+        peer = at_z(i)
+        remote(cm_send.at[peer], cm_recv.at[z], MASSES, (other, peer, b)).start()
+    for copy in halo[2:]:
+        copy.start()
+    for i in far_first[5:]:
+        peer = at_z(i)
+        remote(cm_send.at[peer], cm_recv.at[z], MASSES, (other, peer, b)).start()
+
+    pl.when(late)(prepare)
     for copy in halo[:2]:
         copy.wait()
     quarter = lane & 3
@@ -277,7 +283,21 @@
     change_w = packed(halo_w, own_w, own_w2, betas(c_w, c_w_next))
     change_e = packed(own_e2, own_e, halo_e, betas(c_e, c_e_next))
 
-    for copy in halo[2:]:
+    for f in range(F):
+        value = base[f] - jnp.where(lane < 4, left(change_w, 4 * f), 0.0)
+        base[f] = value - jnp.where(lane >= 124, left(change_e, 4 * f + 4), 0.0)
+
+    halo[4].wait()
+
+    @pl.when(z == nz - 1)
+    def _():
+        clat[:, 8:9, :] = jnp.zeros((L, 1, C), F32)
+
+    for l in range(L):
+        for k, coef in enumerate(betas(clat[l, 0:8, :], clat[l, 1:9, :])):
+            latw[l, k] = coef
+
+    for copy in halo[2:4]:
         copy.wait()
 
     @pl.when(z == 0)
@@ -287,18 +307,15 @@
     @pl.when(z == nz - 1)
     def _():
         field[:, 16:19, :] = jnp.zeros((F, 3, C), F32)
-        clat[:, 8:9, :] = jnp.zeros((L, 1, C), F32)
 
     keep = filled < 0.5
     mass_new = [jnp.zeros((R, C), F32) for _ in range(T)]
     for l in range(L):
-        coef = betas(clat[l, 0:8, :], clat[l, 1:9, :])
+        coef = [latw[l, k] for k in range(7)]
         kept = jnp.where(keep, mass[l * R : (l + 1) * R, :], 0.0)
         for t in range(T):
             f = t * L + l
             value = base[f]
-            value -= jnp.where(lane < 4, left(change_w, 4 * f), 0.0)
-            value -= jnp.where(lane >= 124, left(change_e, 4 * f + 4), 0.0)
             for k in range(7):
                 value -= coef[k] * field[f, 5 + k : 13 + k, :]
             adv[f * R : (f + 1) * R, :] = value
@@ -334,26 +351,20 @@
         mass_new[half] += jnp.where(low, parts[half], 0.0)
         mass_new[half + 2] += jnp.where(low, 0.0, parts[half])
     stacked = jnp.concatenate(
-        [jnp.sum(m, axis=0, keepdims=True) for m in mass_old + mass_new], axis=0
+        [jnp.sum(m, axis=0, keepdims=True) for m in [mass_old[t] for t in range(T)] + mass_new], axis=0
     )
     sums = jnp.sum(stacked, axis=1, keepdims=True)
     row = jnp.sum(jnp.where(lane == sub[0:R, :], sums, 0.0), axis=0, keepdims=True)
 
-    rows[0] = row
-    group = [(other, z, b)]
-    group += [(core, z, at_x(i)) for i in range(1, NX) for core in (p, other)]
-    for i, device in enumerate(group):
-        remote(rows.at[0], sum_x.at[i], SUM_X, device).start()
-    wait_all(sum_x, recv_sem.at[SUM_X])
-    row = row + jnp.sum(sum_x[...], axis=0)
-    rows[1] = row
-    for i in range(1, ny):
-        remote(rows.at[1], sum_y.at[i - 1], SUM_Y, (p, z, at_y(i))).start()
-    wait_all(sum_y, recv_sem.at[SUM_Y])
-    row = row + jnp.sum(sum_y[...], axis=0)
-    rows[2] = row
-    for i in range(1, nz):
-        remote(rows.at[2], sum_z.at[i - 1], SUM_Z, (p, at_z(i), b)).start()
+    rows[0:1, :] = row
+    for n, (i, j) in enumerate(plane):
+        remote(rows.at[pl.ds(0, 1), :], sum_xy.at[pl.ds(n, 1), :], SUM_XY, (p, z, at_plane(i, j))).start()
+    wait_all(sum_xy, recv_sem.at[SUM_XY])
+    row = row + jnp.sum(sum_xy[...], axis=0, keepdims=True)
+    rows[1:2, :] = row
+    line = [(core, i) for i in far_first if i > 0 for core in (p, other)] + [(other, 0)]
+    for n, (core, i) in enumerate(line):
+        remote(rows.at[pl.ds(1, 1), :], sum_z.at[pl.ds(n, 1), :], SUM_Z, (core, at_z(i), b)).start()
 
     wait_all(arrived, recv_sem.at[MARGIN])
     for v in range(6):
@@ -378,15 +389,14 @@
         out[f] = jnp.where(keep, adv[at, :], scattered[pl.ds(f, R, stride=F), :])
 
     wait_all(sum_z, recv_sem.at[SUM_Z])
-    row = row + jnp.sum(sum_z[...], axis=0)
+    row = row + jnp.sum(sum_z[...], axis=0, keepdims=True)
     ratio = row / left(row, 4)
     for t in range(T):
         scale_out[t] = jnp.broadcast_to(ratio[:, t : t + 1], (R, C))
 
     wait_all(cm_send, send_sem.at[MASSES])
     wait_all(packet, send_sem.at[MARGIN])
-    wait_all(sum_x, send_sem.at[SUM_X])
-    wait_all(sum_y, send_sem.at[SUM_Y])
+    wait_all(sum_xy, send_sem.at[SUM_XY])
     wait_all(sum_z, send_sem.at[SUM_Z])
 
 
@@ -427,11 +437,12 @@
                 pltpu.VMEM((nz, 4, C), F32),
                 pltpu.VMEM((nz, 2 * R, C), F32),
                 pltpu.VMEM((nz, 2 * R, C), F32),
-                pltpu.VMEM((3, 1, C), F32),
-                pltpu.VMEM((2 * NX - 1, 1, C), F32),
-                pltpu.VMEM((ny - 1, 1, C), F32),
-                pltpu.VMEM((nz - 1, 1, C), F32),
+                pltpu.VMEM((2, C), F32),
+                pltpu.VMEM((nlon - 1, C), F32),
+                pltpu.VMEM((2 * nz - 1, C), F32),
+                pltpu.VMEM((T, R, C), F32),
                 pltpu.VMEM((F, R, C), F32),
+                pltpu.VMEM((L, 7, R, C), F32),
                 pltpu.VMEM((F * R, C), F32),
                 pltpu.VMEM((C, slots), BF16),
                 pltpu.VMEM((3 * C, slots), BF16),
@@ -443,8 +454,8 @@
                 pltpu.VMEM((2 * R, slots), BF16),
                 pltpu.VMEM((F * R, C), F32),
                 pltpu.SemaphoreType.DMA((8,)),
-                pltpu.SemaphoreType.DMA((10,)),
-                pltpu.SemaphoreType.DMA((10,)),
+                pltpu.SemaphoreType.DMA((9,)),
+                pltpu.SemaphoreType.DMA((9,)),
             ],
             compiler_params=pltpu.CompilerParams(collective_id=0, has_side_effects=True),
         )(

time: 39 us -> 38.2 us (0.979)
  Pallas kernels: 38.1 us -> 37.3 us
    pallas_call x1, Pallas kernels: 38.1 us -> 37.3 us  [body(): pl.pallas_call(run, out_shape=(pltpu.VMEM((F, R, C), F32), pltpu.VMEM((T,...]
where the time goes in v4:
time: 38.2 us; the launch traced here: 38 us
  Pallas kernels  37.3 us (98%)
  other arithmetic  0.67 us (2%)
    pallas_call x1, Pallas kernels, body(): pl.pallas_call(run, out_shape=(pltpu.VMEM((F, R, C), F32), pltpu.VMEM((T,...  37.3 us

profile of v4, /device:TPU:1, one launch (start us, length us, event | category | flops | bytes accessed | tf_op | source)
XLA Modules:
  0.0 38.0 jit_solution(10543317618559664209)
XLA Ops:
  0.0 37.3 %shard_map.82 = (f32[32,8,128]{2,1,0:T(8,128)S(1)}, f32[4,8,128]{2,1,0:T(8,128)S(1)}) custom-call(f32[32,8,128]{2,1,0:T(8,128)} %bitcast.10, f32[8,8,128]{2,1,0:T(8,128)} %bitcast.11, f32[8,8,128]{2,1,0:T(8,128)} %bitcast.12, f32[64,128]{1,0:T(8,128)} %bitcast.13, s32[12,1,64]{2,1,0:T(1,128)} %bitcast.15, f32[2,12,1,64]{3,2,1,0:T(1,128)} %bitcast.14, ...), custom_call_target="tpu_custom_call" | custom-call | tf_op jit(solution)/shard_map/pallas_call | solution.py:415
  37.4 0.7 %broadcast_multiply_fusion = f32[1,4,8,8,128]{4,3,2,1,0:T(8,128)} fusion(f32[1,4,8,8,128]{4,3,2,1,0:T(8,128)S(1)} %bitcast.9, f32[4,8,128]{2,1,0:T(8,128)S(1)} %get-tuple-element.8), kind=kLoop, calls=%fused_computation | loop fusion | flops 32768 | bytes 278528 | tf_op jit(solution)/shard_map/mul | solution.py:471

commit v5 on v4

--- a/solution.py
+++ b/solution.py
@@ -15,8 +15,9 @@
 R = 8
 C = 128
 K = 64
+FAR = 5
 NX = 4
-WEST, EAST, SOUTH, NORTH, NORTH_C, MASSES, MARGIN, SUM_XY, SUM_Z = range(9)
+WEST, EAST, SOUTH, NORTH, NORTH_C, MASSES, MARGIN, SUM_FAR, SUM_NEAR, SUM_Z, DIRECT = range(11)
 
 
 def left(x, by):
@@ -82,7 +83,7 @@
 
 def kernel(nz, nlon, q_hbm, clon_hbm, clat_hbm, mass_hbm, donor_hbm, frac_hbm, target_hbm, live_hbm,
            out, scale_out, field, clon, clat, mass, donor, frac, target, live, send_w, send_e, recv_w, recv_e,
-           cm_send, cm_recv, packet, arrived, rows, sum_xy, sum_z, mass_old, base, latw, adv, onehot, colw,
+           cm_send, cm_recv, packet, arrived, rows, sum_far, sum_near, direct, sum_z, mass_old, base, latw, adv, onehot, colw,
            roww, lhs, mixed, scat_hi, scat_lo, rowmask, scattered, local_sem, send_sem, recv_sem):
     p = lax.axis_index("panel")
     z = lax.axis_index("lat")
@@ -119,8 +120,26 @@
     partners += [(p, z, at_plane(i, j)) for i, j in plane]
     for load in (loads[6], loads[7], loads[3], *loads[:3], *loads[4:6]):
         load.start()
+    middle = range(4, nz - 3)
+    is_first = (p == 1) & (z == 0) & (b == 0)
+    in_middle = (z >= middle[0]) & (z <= middle[-1])
+    sends_direct = [(at_plane(i, j) == 0) & in_middle for i, j in plane[:FAR]]
+    direct_any = sends_direct[0]
+    for one in sends_direct[1:]:
+        direct_any = direct_any | one
+
     for partner in partners:
         pl.semaphore_signal(barrier, inc=1, device_id=partner, device_id_type=MESH)
+
+    @pl.when(is_first)
+    def _():
+        for i, j in plane[:FAR]:
+            place = (ny - i) % ny * NX + (NX - j) % NX
+
+            @pl.loop(middle[0], middle[-1] + 1)
+            def _(level):
+                for core in range(2):
+                    pl.semaphore_signal(barrier, inc=1, device_id=(core, level, place), device_id_type=MESH)
 
     lane = lax.broadcasted_iota(jnp.int32, (R, C), 1)
     lane16 = lax.broadcasted_iota(jnp.int32, (2 * R, C), 1)
@@ -227,7 +246,7 @@
 
     late = z >= nz - 4
     pl.when(jnp.logical_not(late))(prepare)
-    pl.semaphore_wait(barrier, len(partners))
+    pl.semaphore_wait(barrier, len(partners) + jnp.where(direct_any, 1, 0))
 
     def remote(src, dst, which, device):
         return pltpu.make_async_remote_copy(
@@ -357,14 +376,43 @@
     row = jnp.sum(jnp.where(lane == sub[0:R, :], sums, 0.0), axis=0, keepdims=True)
 
     rows[0:1, :] = row
+    rows[3:4, :] = jnp.zeros((1, C), F32)
     for n, (i, j) in enumerate(plane):
-        remote(rows.at[pl.ds(0, 1), :], sum_xy.at[pl.ds(n, 1), :], SUM_XY, (p, z, at_plane(i, j))).start()
-    wait_all(sum_xy, recv_sem.at[SUM_XY])
-    row = row + jnp.sum(sum_xy[...], axis=0, keepdims=True)
+        device = (p, z, at_plane(i, j))
+        if n < FAR:
+            remote(rows.at[pl.ds(0, 1), :], sum_far.at[pl.ds(n, 1), :], SUM_FAR, device).start()
+
+            @pl.when(sends_direct[n])
+            def _():
+                slot = (z - middle[0]) * 2 + p
+                remote(rows.at[pl.ds(0, 1), :], direct.at[slot, pl.ds(n, 1), :], DIRECT, (1, 0, 0)).start()
+
+        else:
+            remote(rows.at[pl.ds(0, 1), :], sum_near.at[pl.ds(n - FAR, 1), :], SUM_NEAR, device).start()
+    line = [(core, i) for i in far_first if i > 0 for core in (p, other)] + [(other, 0)]
+    to_first = [(core == 1) & (b == 0) & (z == nz - i) if i in middle else None for core, i in line]
+    wait_all(sum_near, recv_sem.at[SUM_NEAR])
+    row = row + jnp.sum(sum_near[...], axis=0, keepdims=True)
+    rows[2:3, :] = row
+
+    def along_z(n, source):
+        core, i = line[n]
+        remote(rows.at[pl.ds(source, 1), :], sum_z.at[pl.ds(n, 1), :], SUM_Z, (core, at_z(i), b)).start()
+
+    @pl.when((b == 0) & in_middle)
+    def _():
+        for n, special in enumerate(to_first):
+            if special is not None:
+                pl.when(special)(lambda n=n: along_z(n, 2))
+
+    wait_all(sum_far, recv_sem.at[SUM_FAR])
+    row = row + jnp.sum(sum_far[...], axis=0, keepdims=True)
     rows[1:2, :] = row
-    line = [(core, i) for i in far_first if i > 0 for core in (p, other)] + [(other, 0)]
-    for n, (core, i) in enumerate(line):
-        remote(rows.at[pl.ds(1, 1), :], sum_z.at[pl.ds(n, 1), :], SUM_Z, (core, at_z(i), b)).start()
+    for n, special in enumerate(to_first):
+        if special is None:
+            along_z(n, 1)
+        else:
+            pl.when(jnp.logical_not(special))(lambda n=n: along_z(n, 1))
 
     wait_all(arrived, recv_sem.at[MARGIN])
     for v in range(6):
@@ -388,15 +436,26 @@
         at = pl.ds(f * R, R)
         out[f] = jnp.where(keep, adv[at, :], scattered[pl.ds(f, R, stride=F), :])
 
+    @pl.when(is_first)
+    def _():
+        wait_all(direct, recv_sem.at[DIRECT])
+        rows[3:4, :] = jnp.sum(jnp.sum(direct[...], axis=0), axis=0, keepdims=True)
+
     wait_all(sum_z, recv_sem.at[SUM_Z])
-    row = row + jnp.sum(sum_z[...], axis=0, keepdims=True)
+    row = row + (jnp.sum(sum_z[...], axis=0, keepdims=True) + rows[3:4, :])
     ratio = row / left(row, 4)
     for t in range(T):
         scale_out[t] = jnp.broadcast_to(ratio[:, t : t + 1], (R, C))
 
     wait_all(cm_send, send_sem.at[MASSES])
     wait_all(packet, send_sem.at[MARGIN])
-    wait_all(sum_xy, send_sem.at[SUM_XY])
+    wait_all(sum_far, send_sem.at[SUM_FAR])
+    wait_all(sum_near, send_sem.at[SUM_NEAR])
+
+    @pl.when(direct_any)
+    def _():
+        wait_all(rows.at[pl.ds(0, 1), :], send_sem.at[DIRECT])
+
     wait_all(sum_z, send_sem.at[SUM_Z])
 
 
@@ -437,8 +496,10 @@
                 pltpu.VMEM((nz, 4, C), F32),
                 pltpu.VMEM((nz, 2 * R, C), F32),
                 pltpu.VMEM((nz, 2 * R, C), F32),
-                pltpu.VMEM((2, C), F32),
-                pltpu.VMEM((nlon - 1, C), F32),
+                pltpu.VMEM((4, C), F32),
+                pltpu.VMEM((FAR, C), F32),
+                pltpu.VMEM((nlon - 1 - FAR, C), F32),
+                pltpu.VMEM((2 * (nz - 7), FAR, C), F32),
                 pltpu.VMEM((2 * nz - 1, C), F32),
                 pltpu.VMEM((T, R, C), F32),
                 pltpu.VMEM((F, R, C), F32),
@@ -454,8 +515,8 @@
                 pltpu.VMEM((2 * R, slots), BF16),
                 pltpu.VMEM((F * R, C), F32),
                 pltpu.SemaphoreType.DMA((8,)),
-                pltpu.SemaphoreType.DMA((9,)),
-                pltpu.SemaphoreType.DMA((9,)),
+                pltpu.SemaphoreType.DMA((11,)),
+                pltpu.SemaphoreType.DMA((11,)),
             ],
             compiler_params=pltpu.CompilerParams(collective_id=0, has_side_effects=True),
         )(

time: 38.2 us -> 37.2 us (0.974)
  Pallas kernels: 37.3 us -> 36.4 us
    pallas_call x1, Pallas kernels: 37.3 us -> 36.4 us  [body(): pl.pallas_call(run, out_shape=(pltpu.VMEM((F, R, C), F32), pltpu.VMEM((T,...]
where the time goes in v5:
time: 37.2 us; the launch traced here: 37 us
  Pallas kernels  36.4 us (98%)
  other arithmetic  0.67 us (2%)
    pallas_call x1, Pallas kernels, body(): pl.pallas_call(run, out_shape=(pltpu.VMEM((F, R, C), F32), pltpu.VMEM((T,...  36.4 us

profile of v5, /device:TPU:1, one launch (start us, length us, event | category | flops | bytes accessed | tf_op | source)
XLA Modules:
  0.0 37.0 jit_solution(11423853342383342890)
XLA Ops:
  0.0 36.4 %shard_map.82 = (f32[32,8,128]{2,1,0:T(8,128)S(1)}, f32[4,8,128]{2,1,0:T(8,128)S(1)}) custom-call(f32[32,8,128]{2,1,0:T(8,128)} %bitcast.10, f32[8,8,128]{2,1,0:T(8,128)} %bitcast.11, f32[8,8,128]{2,1,0:T(8,128)} %bitcast.12, f32[64,128]{1,0:T(8,128)} %bitcast.13, s32[12,1,64]{2,1,0:T(1,128)} %bitcast.15, f32[2,12,1,64]{3,2,1,0:T(1,128)} %bitcast.14, ...), custom_call_target="tpu_custom_call" | custom-call | tf_op jit(solution)/shard_map/pallas_call | solution.py:474
  36.4 0.7 %broadcast_multiply_fusion = f32[1,4,8,8,128]{4,3,2,1,0:T(8,128)} fusion(f32[1,4,8,8,128]{4,3,2,1,0:T(8,128)S(1)} %bitcast.9, f32[4,8,128]{2,1,0:T(8,128)S(1)} %get-tuple-element.8), kind=kLoop, calls=%fused_computation | loop fusion | flops 32768 | bytes 278528 | tf_op jit(solution)/shard_map/mul | solution.py:532

commit v6 on v5

--- a/solution.py
+++ b/solution.py
@@ -15,7 +15,7 @@
 R = 8
 C = 128
 K = 64
-FAR = 5
+FAR = 12
 NX = 4
 WEST, EAST, SOUTH, NORTH, NORTH_C, MASSES, MARGIN, SUM_FAR, SUM_NEAR, SUM_Z, DIRECT = range(11)
 
@@ -82,8 +82,8 @@
 
 
 def kernel(nz, nlon, q_hbm, clon_hbm, clat_hbm, mass_hbm, donor_hbm, frac_hbm, target_hbm, live_hbm,
-           out, scale_out, field, clon, clat, mass, donor, frac, target, live, send_w, send_e, recv_w, recv_e,
-           cm_send, cm_recv, packet, arrived, rows, sum_far, sum_near, direct, sum_z, mass_old, base, latw, adv, onehot, colw,
+           out, field, clon, clat, mass, donor, frac, target, live, send_w, send_e, recv_w, recv_e,
+           cm_send, cm_recv, packet, arrived, rows, sum_far, sum_near, direct, sum_z, ends, filled, mass_old, base, latw, adv, onehot, colw,
            roww, lhs, mixed, scat_hi, scat_lo, rowmask, scattered, local_sem, send_sem, recv_sem):
     p = lax.axis_index("panel")
     z = lax.axis_index("lat")
@@ -166,10 +166,6 @@
     for v in range(6):
         cols = pl.ds(v * C, C)
         onehot[:, cols] = jnp.where(column == spot_col[v : v + 1, :], 1.0, 0.0).astype(BF16)
-        rowmask[:, cols] = jnp.where(sub == live_rows[v], 1.0, 0.0).astype(BF16)
-    filled = lax.dot_general(
-        rowmask[...], onehot[...], (((1,), (1,)), ((), ())), preferred_element_type=F32
-    )[0:R, :]
 
     loads[3].wait()
     by_row = jnp.concatenate([mass[pl.ds(r, L, stride=R), :] for r in range(R)], axis=0)
@@ -190,24 +186,28 @@
     loads[0].wait()
     loads[1].wait()
     loads[2].wait()
-    own = [jnp.zeros((R, C), F32) for _ in range(4)]
-    firsts = (0, 4, 124, 120)
-    for f in range(F):
-        tile = field[f, R : 2 * R, :]
-        band = (lane >= 4 * f) & (lane < 4 * f + 4)
-        own = [jnp.where(band, left(tile, first - 4 * f), o) for first, o in zip(firsts, own)]
-    own_w, own_w2, own_e, own_e2 = own
-    edge = [jnp.zeros((R, C), F32) for _ in range(4)]
-    firsts = (0, 1, 124, 125)
-    for l in range(L):
-        tile = clon[l]
-        band = (lane >= 4 * l) & (lane < 4 * l + 4)
-        edge = [jnp.where(band, left(tile, first - 4 * l), o) for first, o in zip(firsts, edge)]
-    edge = [o + pltpu.roll(o, 32, 1) for o in edge]
-    c_w, c_w_next, c_e, c_e_next = [o + pltpu.roll(o, 64, 1) for o in edge]
-    send_w[0] = own_w
-    send_w[1] = c_w
-    send_e[0] = own_e
+
+    def pack_ends():
+        own = [jnp.zeros((R, C), F32) for _ in range(4)]
+        firsts = (0, 4, 124, 120)
+        for f in range(F):
+            tile = field[f, R : 2 * R, :]
+            band = (lane >= 4 * f) & (lane < 4 * f + 4)
+            own = [jnp.where(band, left(tile, first - 4 * f), o) for first, o in zip(firsts, own)]
+        edge = [jnp.zeros((R, C), F32) for _ in range(4)]
+        firsts = (0, 1, 124, 125)
+        for l in range(L):
+            tile = clon[l]
+            band = (lane >= 4 * l) & (lane < 4 * l + 4)
+            edge = [jnp.where(band, left(tile, first - 4 * l), o) for first, o in zip(firsts, edge)]
+        edge = [o + pltpu.roll(o, 32, 1) for o in edge]
+        edge = [o + pltpu.roll(o, 64, 1) for o in edge]
+        for n, tile in enumerate(own + edge):
+            ends[n] = tile
+        send_w[0] = own[0]
+        send_w[1] = edge[0]
+        send_e[0] = own[2]
+
     def prepare():
         loads[4].wait()
         loads[5].wait()
@@ -228,6 +228,12 @@
             colw[C : 2 * C, cols] = high
             colw[2 * C : 3 * C, cols] = low_part
 
+        for v in range(6):
+            rowmask[:, pl.ds(v * C, C)] = jnp.where(sub == live_rows[v], 1.0, 0.0).astype(BF16)
+        filled[...] = lax.dot_general(
+            rowmask[...], onehot[...], (((1,), (1,)), ((), ())), preferred_element_type=F32
+        )[0:R, :]
+
         inside = (lane >= 4) & (lane < 124)
         old = [jnp.zeros((R, C), F32) for _ in range(T)]
         for l in range(L):
@@ -244,7 +250,9 @@
         for t in range(T):
             mass_old[t] = old[t]
 
-    late = z >= nz - 4
+    pack_ends()
+
+    late = (z >= nz - 2) & (y >= ny // 2) & (y < ny - 1)
     pl.when(jnp.logical_not(late))(prepare)
     pl.semaphore_wait(barrier, len(partners) + jnp.where(direct_any, 1, 0))
 
@@ -266,20 +274,24 @@
         remote(field.at[:, pl.ds(8, 3), :], field.at[:, pl.ds(16, 3), :], NORTH, (p, south, b)),
         remote(clat.at[:, pl.ds(0, 1), :], clat.at[:, pl.ds(R, 1), :], NORTH_C, (p, south, b)),
     ]
-    for copy in halo[:2]:
-        copy.start()
-    for i in far_first[:5]:
-        peer = at_z(i)
-        remote(cm_send.at[peer], cm_recv.at[z], MASSES, (other, peer, b)).start()
-    for copy in halo[2:]:
-        copy.start()
-    for i in far_first[5:]:
-        peer = at_z(i)
-        remote(cm_send.at[peer], cm_recv.at[z], MASSES, (other, peer, b)).start()
-
+    def send_masses(steps):
+        for i in steps:
+            peer = at_z(i)
+            remote(cm_send.at[peer], cm_recv.at[z], MASSES, (other, peer, b)).start()
+
+    def start(copies):
+        for copy in copies:
+            copy.start()
+
+    start(halo[:2])
+    send_masses(far_first[:5])
+    start(halo[2:])
+    send_masses(far_first[5:])
     pl.when(late)(prepare)
+
     for copy in halo[:2]:
         copy.wait()
+    own_w, own_w2, own_e, own_e2, c_w, c_w_next, c_e, c_e_next = (ends[n] for n in range(8))
     quarter = lane & 3
     halo_w = jnp.where(b == 0, 0.0, recv_w[0])
     halo_e = jnp.where(b == nlon - 1, 0.0, recv_e[0])
@@ -327,7 +339,7 @@
     def _():
         field[:, 16:19, :] = jnp.zeros((F, 3, C), F32)
 
-    keep = filled < 0.5
+    keep = filled[...] < 0.5
     mass_new = [jnp.zeros((R, C), F32) for _ in range(T)]
     for l in range(L):
         coef = [latw[l, k] for k in range(7)]
@@ -434,7 +446,7 @@
     ) + lax.dot_general(scat_lo[...], onehot[...], nt, preferred_element_type=F32)
     for f in range(F):
         at = pl.ds(f * R, R)
-        out[f] = jnp.where(keep, adv[at, :], scattered[pl.ds(f, R, stride=F), :])
+        adv[at, :] = jnp.where(keep, adv[at, :], scattered[pl.ds(f, R, stride=F), :])
 
     @pl.when(is_first)
     def _():
@@ -445,7 +457,10 @@
     row = row + (jnp.sum(sum_z[...], axis=0, keepdims=True) + rows[3:4, :])
     ratio = row / left(row, 4)
     for t in range(T):
-        scale_out[t] = jnp.broadcast_to(ratio[:, t : t + 1], (R, C))
+        scale = jnp.broadcast_to(ratio[:, t : t + 1], (R, C))
+        for l in range(L):
+            f = t * L + l
+            out[f] = adv[f * R : (f + 1) * R, :] * scale
 
     wait_all(cm_send, send_sem.at[MASSES])
     wait_all(packet, send_sem.at[MARGIN])
@@ -471,14 +486,11 @@
         def run(*refs):
             kernel(nz, nlon, *refs)
 
-        merged, scale = pl.pallas_call(
+        result = pl.pallas_call(
             run,
-            out_shape=(
-                pltpu.VMEM((F, R, C), F32),
-                pltpu.VMEM((T, R, C), F32),
-            ),
+            out_shape=pltpu.VMEM((F, R, C), F32),
             in_specs=[hbm_spec] * 8,
-            out_specs=(vmem_spec, vmem_spec),
+            out_specs=vmem_spec,
             scratch_shapes=[
                 pltpu.VMEM((F, 3 * R, C), F32),
                 pltpu.VMEM((L, R, C), F32),
@@ -501,6 +513,8 @@
                 pltpu.VMEM((nlon - 1 - FAR, C), F32),
                 pltpu.VMEM((2 * (nz - 7), FAR, C), F32),
                 pltpu.VMEM((2 * nz - 1, C), F32),
+                pltpu.VMEM((8, R, C), F32),
+                pltpu.VMEM((R, C), F32),
                 pltpu.VMEM((T, R, C), F32),
                 pltpu.VMEM((F, R, C), F32),
                 pltpu.VMEM((L, 7, R, C), F32),
@@ -529,7 +543,7 @@
             target_cell.reshape(nz, 1, K),
             live_count.reshape(nz),
         )
-        return merged.reshape(1, T, L, R, C) * scale.reshape(1, T, 1, R, C)
+        return result.reshape(1, T, L, R, C)
 
     lon = "lon"
     placed = (

time: 37.2 us -> 36.8 us (0.989)
  other arithmetic: 0.67 us -> 0 us
  local copies, waits for them, and re-layouts: 0 us -> 0.66 us
  Pallas kernels: 36.4 us -> 36 us
    mul x1 -> x0, other arithmetic: 0.67 us -> none  [body(): return merged.reshape(1, T, L, R, C) * scale.reshape(1, T, 1, R, C)]
    unnamed x0 -> x1, local copies, waits for them, and re-layouts: none -> 0.66 us
    pallas_call x1, Pallas kernels: 36.4 us -> 36 us  [body(): pl.pallas_call(run, out_shape=pltpu.VMEM((F, R, C), F32), in_specs=[hbm_s...]
where the time goes in v6:
time: 36.8 us; the launch traced here: 36.6 us
  Pallas kernels  36 us (98%)
  local copies, waits for them, and re-layouts  0.66 us (2%)
    pallas_call x1, Pallas kernels, body(): pl.pallas_call(run, out_shape=pltpu.VMEM((F, R, C), F32), in_specs=[hbm_s...  36 us

profile of v6, /device:TPU:1, one launch (start us, length us, event | category | flops | bytes accessed | tf_op | source)
XLA Modules:
  0.0 36.6 jit_solution(1603330343719042829)
XLA Ops:
  0.0 36.0 %shard_map.82 = f32[32,8,128]{2,1,0:T(8,128)S(1)} custom-call(f32[32,8,128]{2,1,0:T(8,128)} %bitcast.10, f32[8,8,128]{2,1,0:T(8,128)} %bitcast.11, f32[8,8,128]{2,1,0:T(8,128)} %bitcast.12, f32[64,128]{1,0:T(8,128)} %bitcast.13, s32[12,1,64]{2,1,0:T(1,128)} %bitcast.15, f32[2,12,1,64]{3,2,1,0:T(1,128)} %bitcast.14, s32[12,1,64]{2,1,0:T(1,128)} %bitcast.16, ...), custom_call_target="tpu_custom_call" | custom-call | tf_op jit(solution)/shard_map/pallas_call | solution.py:489
  36.0 0.7 %copy.10 = f32[1,4,8,8,128]{4,3,2,1,0:T(8,128)} copy(f32[1,4,8,8,128]{4,3,2,1,0:T(8,128)S(1)} %bitcast.9) | data formatting | bytes 262144

commit v7 on v6

--- a/solution.py
+++ b/solution.py
@@ -120,7 +120,7 @@
     partners += [(p, z, at_plane(i, j)) for i, j in plane]
     for load in (loads[6], loads[7], loads[3], *loads[:3], *loads[4:6]):
         load.start()
-    middle = range(4, nz - 3)
+    middle = range(3, nz - 2)
     is_first = (p == 1) & (z == 0) & (b == 0)
     in_middle = (z >= middle[0]) & (z <= middle[-1])
     sends_direct = [(at_plane(i, j) == 0) & in_middle for i, j in plane[:FAR]]
@@ -511,7 +511,7 @@
                 pltpu.VMEM((4, C), F32),
                 pltpu.VMEM((FAR, C), F32),
                 pltpu.VMEM((nlon - 1 - FAR, C), F32),
-                pltpu.VMEM((2 * (nz - 7), FAR, C), F32),
+                pltpu.VMEM((2 * (nz - 5), FAR, C), F32),
                 pltpu.VMEM((2 * nz - 1, C), F32),
                 pltpu.VMEM((8, R, C), F32),
                 pltpu.VMEM((R, C), F32),

time: 36.8 us -> 36.8 us (level)
  no operation moved by 1% of the time
where the time goes in v7:
time: 36.8 us; the launch traced here: 36.6 us
  Pallas kernels  36 us (98%)
  local copies, waits for them, and re-layouts  0.66 us (2%)
    pallas_call x1, Pallas kernels, body(): pl.pallas_call(run, out_shape=pltpu.VMEM((F, R, C), F32), in_specs=[hbm_s...  36 us

profile of v7, /device:TPU:1, one launch (start us, length us, event | category | flops | bytes accessed | tf_op | source)
XLA Modules:
  0.0 36.6 jit_solution(13592260673051013508)
XLA Ops:
  0.0 36.0 %shard_map.82 = f32[32,8,128]{2,1,0:T(8,128)S(1)} custom-call(f32[32,8,128]{2,1,0:T(8,128)} %bitcast.10, f32[8,8,128]{2,1,0:T(8,128)} %bitcast.11, f32[8,8,128]{2,1,0:T(8,128)} %bitcast.12, f32[64,128]{1,0:T(8,128)} %bitcast.13, s32[12,1,64]{2,1,0:T(1,128)} %bitcast.15, f32[2,12,1,64]{3,2,1,0:T(1,128)} %bitcast.14, s32[12,1,64]{2,1,0:T(1,128)} %bitcast.16, ...), custom_call_target="tpu_custom_call" | custom-call | tf_op jit(solution)/shard_map/pallas_call | solution.py:489
  36.0 0.7 %copy.10 = f32[1,4,8,8,128]{4,3,2,1,0:T(8,128)} copy(f32[1,4,8,8,128]{4,3,2,1,0:T(8,128)S(1)} %bitcast.9) | data formatting | bytes 262144

commit v8 on v7

--- a/solution.py
+++ b/solution.py
@@ -370,6 +370,18 @@
         peer = at_z(i)
         remote(packet.at[peer], arrived.at[z], MARGIN, (other, peer, b)).start()
 
+    def spread(stacked, first):
+        sums = jnp.sum(stacked, axis=1, keepdims=True)
+        count = stacked.shape[0]
+        return jnp.sum(
+            jnp.where(lane[0:count, :] == sub[0:count, :] + first, sums, 0.0), axis=0, keepdims=True
+        )
+
+    masses = [mass_old[t] for t in range(T)] + mass_new
+    rows[2:3, :] = spread(
+        jnp.concatenate([jnp.sum(m, axis=0, keepdims=True) for m in masses], axis=0), 0
+    )
+
     wait_all(cm_recv, recv_sem.at[MASSES])
     parts = [jnp.zeros((R, C), F32) for _ in range(2)]
     for d in range(12):
@@ -378,14 +390,10 @@
         eight = jnp.where(low, eight, left(eight, K))
         for half in range(2):
             parts[half] += eight * packet[d, half * R : (half + 1) * R, :]
-    for half in range(2):
-        mass_new[half] += jnp.where(low, parts[half], 0.0)
-        mass_new[half + 2] += jnp.where(low, 0.0, parts[half])
-    stacked = jnp.concatenate(
-        [jnp.sum(m, axis=0, keepdims=True) for m in [mass_old[t] for t in range(T)] + mass_new], axis=0
-    )
-    sums = jnp.sum(stacked, axis=1, keepdims=True)
-    row = jnp.sum(jnp.where(lane == sub[0:R, :], sums, 0.0), axis=0, keepdims=True)
+    parts = [jnp.sum(part, axis=0, keepdims=True) for part in parts]
+    halved = [jnp.where(lane_row < K, part, 0.0) for part in parts]
+    halved += [jnp.where(lane_row < K, 0.0, part) for part in parts]
+    row = rows[2:3, :] + spread(jnp.concatenate(halved, axis=0), T)
 
     rows[0:1, :] = row
     rows[3:4, :] = jnp.zeros((1, C), F32)

time: 36.8 us -> 36.8 us (level)
  no operation moved by 1% of the time
where the time goes in v8:
time: 36.8 us; the launch traced here: 36.7 us
  Pallas kernels  36 us (98%)
  local copies, waits for them, and re-layouts  0.66 us (2%)
    pallas_call x1, Pallas kernels, body(): pl.pallas_call(run, out_shape=pltpu.VMEM((F, R, C), F32), in_specs=[hbm_s...  36 us

profile of v8, /device:TPU:1, one launch (start us, length us, event | category | flops | bytes accessed | tf_op | source)
XLA Modules:
  0.0 36.7 jit_solution(12299546133255255852)
XLA Ops:
  0.0 36.0 %shard_map.82 = f32[32,8,128]{2,1,0:T(8,128)S(1)} custom-call(f32[32,8,128]{2,1,0:T(8,128)} %bitcast.10, f32[8,8,128]{2,1,0:T(8,128)} %bitcast.11, f32[8,8,128]{2,1,0:T(8,128)} %bitcast.12, f32[64,128]{1,0:T(8,128)} %bitcast.13, s32[12,1,64]{2,1,0:T(1,128)} %bitcast.15, f32[2,12,1,64]{3,2,1,0:T(1,128)} %bitcast.14, s32[12,1,64]{2,1,0:T(1,128)} %bitcast.16, ...), custom_call_target="tpu_custom_call" | custom-call | tf_op jit(solution)/shard_map/pallas_call | solution.py:497
  36.0 0.7 %copy.10 = f32[1,4,8,8,128]{4,3,2,1,0:T(8,128)} copy(f32[1,4,8,8,128]{4,3,2,1,0:T(8,128)S(1)} %bitcast.9) | data formatting | bytes 262144
